TPU v7x, 32 devices: a whole 2x2x4 slice. The times are simulated.
32 devices in a mesh: dp: 4 (over z), tensor: 8 (over y, x, core).
Axes of the slice: x: 2, y: 2, z: 4, core: 2. Of those that a mesh axis runs over, the one named last changes fastest.
Arguments:
- tokens: bfloat16 [8192, 1152], P('dp'), may hold values from -6 to 6
- condition: float32 [32, 1152], P('dp'), may hold values from -6 to 6
- timesteps: int32 [32], P('dp'), may hold values from 0 to 999
- route_masks: int32 [1000, 16, 2], P(None, 'tensor'), may hold values 0 or 1
- modulate_weight: bfloat16 [1152, 6, 1152], P(None, None, 'tensor'), may hold values from -0.1875 to 0.1875
- modulate_bias: bfloat16 [6, 1152], P(None, 'tensor'), may hold values from -1.5 to 1.5
- input_weight: bfloat16 [1152, 3, 1152], P(None, None, 'tensor'), may hold values from -0.1875 to 0.1875
- input_bias: bfloat16 [2, 1152], P(None, 'tensor'), may hold values from -1.5 to 1.5
- output_weight: bfloat16 [1152, 1152], P('tensor'), may hold values from -1.5 to 1.5
- output_bias: bfloat16 [1152], replicated, may hold values from -1.5 to 1.5
- expand_weight: bfloat16 [1152, 4608], P(None, 'tensor'), may hold values from -0.1875 to 0.1875
- expand_bias: bfloat16 [4608], P('tensor'), may hold values from -1.5 to 1.5
- reduce_weight: bfloat16 [4608, 1152], P('tensor'), may hold values from -0.1875 to 0.1875
- reduce_bias: bfloat16 [1152], replicated, may hold values from -1.5 to 1.5
- router_weight: bfloat16 [1152, 16, 2], P(None, 'tensor'), may hold values from -0.1875 to 0.1875
- router_bias: bfloat16 [16, 2], P('tensor'), may hold values from -1.2 to 1.2
- out_cotangent: bfloat16 [8192, 1152], P('dp'), may hold values from -6 to 6
Outputs:
- block_output: float32 [8192, 1152], P('dp')
- tokens_grad: float32 [8192, 1152], P('dp')
- modulate_weight_grad: float32 [1152, 6, 1152], P(None, None, 'tensor')
- modulate_bias_grad: float32 [6, 1152], P(None, 'tensor')
- input_weight_grad: float32 [1152, 3, 1152], P(None, None, 'tensor')
- input_bias_grad: float32 [2, 1152], P(None, 'tensor')
- output_weight_grad: float32 [1152, 1152], P('tensor')
- output_bias_grad: float32 [1152], replicated
- expand_weight_grad: float32 [1152, 4608], P(None, 'tensor')
- expand_bias_grad: float32 [4608], P('tensor')
- reduce_weight_grad: float32 [4608, 1152], P('tensor')
- reduce_bias_grad: float32 [1152], replicated
- router_weight_grad: float32 [1152, 16, 2], P(None, 'tensor')
- router_bias_grad: float32 [16, 2], P('tensor')
Inputs may be any that keep to these rules, and one draw needn't show every extreme that they name: `timesteps`: each timestep selects the row of route_masks used by its item.
All inputs are finite; a program needn't handle non-finite values. No bound on the sum of `route_masks` on one device may be relied on, other than what follows from the above.
Results may differ from a plain program's by a relative error of at most 0.013.
The roundings to bfloat16 on the way count: a program that leaves them out, or rounds other values in their place, can miss the bound.
Values may be sent and summed in bfloat16 or wider, within the bound.
A program may use at most 256 MiB of HBM per device.

v0:
```python
import math

import jax
import jax.numpy as jnp
from jax import lax
from jax.sharding import PartitionSpec as P

HIGHEST = lax.Precision.HIGHEST
EPSILON = 1e-06


def layer_norm(values):
    center = values - jnp.mean(values, axis=-1, keepdims=True)
    inverse = lax.rsqrt(jnp.mean(center * center, axis=-1, keepdims=True) + EPSILON)
    return (center * inverse, inverse)


def norm_back(grad_norm, normed, inverse):
    mean_grad = jnp.mean(grad_norm, axis=-1, keepdims=True)
    mean_cross = jnp.mean(grad_norm * normed, axis=-1, keepdims=True)
    return inverse * (grad_norm - mean_grad - normed * mean_cross)


def gelu_tanh(values):
    return jax.nn.gelu(values, approximate=True)


def contract_rows(left, right):
    return lax.dot_general(
        left, right, (((0,), (0,)), ((), ())), preferred_element_type=jnp.float32
    )


def contract_cols(left, right):
    return lax.dot_general(
        left, right, (((1,), (1,)), ((), ())), preferred_element_type=jnp.float32
    )


def body(
    tokens,
    condition,
    timesteps,
    route_masks,
    modulate_weight,
    modulate_bias,
    input_weight,
    input_bias,
    output_weight,
    output_bias,
    expand_weight,
    expand_bias,
    reduce_weight,
    reduce_bias,
    router_weight,
    router_bias,
    out_cotangent,
):
    model_width = tokens.shape[1]
    item_count = condition.shape[0]
    rows_all = tokens.shape[0]
    item_length = rows_all // item_count
    local_heads = router_weight.shape[1]
    local_width = input_weight.shape[2]
    head_size = local_width // local_heads
    group_width = expand_weight.shape[1] // local_heads
    score_scale = 1.0 / math.sqrt(head_size)
    silu_condition = jax.nn.silu(condition).astype(jnp.bfloat16)
    condition_low = condition.astype(jnp.bfloat16)
    modulate_part = jnp.einsum(
        "bd,dke->bke", silu_condition, modulate_weight, preferred_element_type=jnp.float32
    ) + modulate_bias.astype(jnp.float32)
    modulation = lax.all_gather(modulate_part, "tensor", axis=2, tiled=True)
    shift_one, scale_one, gate_one, shift_two, scale_two, gate_two = [
        modulation[:, column][:, None, :] for column in range(6)
    ]
    logits = jnp.einsum(
        "bd,dhc->bhc", condition_low, router_weight, preferred_element_type=jnp.float32
    ) + router_bias.astype(jnp.float32)
    sigmoid_out = jax.nn.sigmoid(logits)
    step_table = (
        timesteps[:, None] == jnp.arange(route_masks.shape[0], dtype=jnp.int32)[None, :]
    ).astype(jnp.float32)
    mask_rows = jnp.einsum(
        "bs,shc->bhc", step_table, route_masks.astype(jnp.float32), precision=HIGHEST
    )
    gate_values = mask_rows * sigmoid_out
    head_gate = gate_values[:, :, 0]
    group_gate = gate_values[:, :, 1]
    inputs_f = tokens.astype(jnp.float32).reshape(item_count, item_length, model_width)
    normed_one, inverse_one = layer_norm(inputs_f)
    hidden_one = (normed_one * (1.0 + scale_one) + shift_one).astype(jnp.bfloat16)
    projected = jnp.einsum(
        "bsd,dke->bske", hidden_one, input_weight, preferred_element_type=jnp.float32
    )
    input_bias_f = input_bias.astype(jnp.float32)
    head_shape = (item_count, item_length, local_heads, head_size)
    queries = (projected[:, :, 0] + input_bias_f[0]).astype(jnp.bfloat16).reshape(head_shape)
    keys_low = projected[:, :, 1].astype(jnp.bfloat16).reshape(head_shape)
    values_low = (projected[:, :, 2] + input_bias_f[1]).astype(jnp.bfloat16).reshape(head_shape)
    scores = (
        jnp.einsum("bqhe,bkhe->bhqk", queries, keys_low, preferred_element_type=jnp.float32)
        * score_scale
    )
    row_max = jnp.max(scores, axis=-1, keepdims=True)
    log_total = row_max + jnp.log(jnp.sum(jnp.exp(scores - row_max), axis=-1, keepdims=True))
    softmax_low = jnp.exp(scores - log_total).astype(jnp.bfloat16)
    mixed_heads = jnp.einsum(
        "bhqk,bkhe->bqhe", softmax_low, values_low, preferred_element_type=jnp.float32
    )
    gated_heads = (
        (mixed_heads * head_gate[:, None, :, None])
        .astype(jnp.bfloat16)
        .reshape(rows_all, local_width)
    )
    attention_part = jnp.dot(gated_heads, output_weight, preferred_element_type=jnp.float32)
    attention = (lax.psum(attention_part, "tensor") + output_bias.astype(jnp.float32)).reshape(
        item_count, item_length, model_width
    )
    residual_one = inputs_f + gate_one * attention
    normed_two, inverse_two = layer_norm(residual_one)
    hidden_two = (
        (normed_two * (1.0 + scale_two) + shift_two)
        .astype(jnp.bfloat16)
        .reshape(rows_all, model_width)
    )
    expanded = jnp.dot(
        hidden_two, expand_weight, preferred_element_type=jnp.float32
    ) + expand_bias.astype(jnp.float32)
    activated = gelu_tanh(expanded)
    group_shape = (item_count, item_length, local_heads, group_width)
    gated_channels = (
        (activated.reshape(group_shape) * group_gate[:, None, :, None])
        .astype(jnp.bfloat16)
        .reshape(rows_all, -1)
    )
    mlp_part = jnp.dot(gated_channels, reduce_weight, preferred_element_type=jnp.float32)
    branch_two = (lax.psum(mlp_part, "tensor") + reduce_bias.astype(jnp.float32)).reshape(
        item_count, item_length, model_width
    )
    block_output = residual_one + gate_two * branch_two
    cotangent = out_cotangent.astype(jnp.float32).reshape(item_count, item_length, model_width)
    gate_two_grad = jnp.sum(cotangent * branch_two, axis=1)
    branch_grad = (gate_two * cotangent).astype(jnp.bfloat16).reshape(rows_all, model_width)
    reduce_bias_grad = jnp.sum(branch_grad.astype(jnp.float32), axis=0)
    reduce_weight_grad = contract_rows(gated_channels, branch_grad)
    channel_blocks = contract_cols(branch_grad, reduce_weight).reshape(group_shape)
    group_gate_grad = jnp.sum(channel_blocks * activated.reshape(group_shape), axis=(1, 3))
    activated_grad = (channel_blocks * group_gate[:, None, :, None]).reshape(rows_all, -1)
    expanded_grad = jax.vjp(gelu_tanh, expanded)[1](activated_grad)[0].astype(jnp.bfloat16)
    expand_bias_grad = jnp.sum(expanded_grad.astype(jnp.float32), axis=0)
    expand_weight_grad = contract_rows(hidden_two, expanded_grad)
    hidden_two_part = contract_cols(expanded_grad, expand_weight)
    hidden_two_grad = lax.psum(hidden_two_part, "tensor").reshape(
        item_count, item_length, model_width
    )
    shift_two_grad = jnp.sum(hidden_two_grad, axis=1)
    scale_two_grad = jnp.sum(hidden_two_grad * normed_two, axis=1)
    residual_grad = cotangent + norm_back(
        hidden_two_grad * (1.0 + scale_two), normed_two, inverse_two
    )
    branch_one_grad = (gate_one * residual_grad).astype(jnp.bfloat16).reshape(rows_all, model_width)
    output_bias_grad = jnp.sum(branch_one_grad.astype(jnp.float32), axis=0)
    output_weight_grad = contract_rows(gated_heads, branch_one_grad)
    heads_grad = contract_cols(branch_one_grad, output_weight).reshape(head_shape)
    head_gate_grad = jnp.sum(heads_grad * mixed_heads, axis=(1, 3))
    mixed_grad = (heads_grad * head_gate[:, None, :, None]).astype(jnp.bfloat16)
    scores_again = (
        jnp.einsum("bqhe,bkhe->bhqk", queries, keys_low, preferred_element_type=jnp.float32)
        * score_scale
    )
    softmax_full = jnp.exp(scores_again - log_total)
    softmax_grad = jnp.einsum(
        "bqhe,bkhe->bhqk", mixed_grad, values_low, preferred_element_type=jnp.float32
    )
    values_grad = jnp.einsum(
        "bhqk,bqhe->bkhe",
        softmax_full.astype(jnp.bfloat16),
        mixed_grad,
        preferred_element_type=jnp.float32,
    )
    score_grad = (
        softmax_full * (softmax_grad - jnp.sum(softmax_grad * softmax_full, axis=-1, keepdims=True))
    ).astype(jnp.bfloat16)
    queries_grad = (
        jnp.einsum("bhqk,bkhe->bqhe", score_grad, keys_low, preferred_element_type=jnp.float32)
        * score_scale
    )
    keys_grad = (
        jnp.einsum("bhqk,bqhe->bkhe", score_grad, queries, preferred_element_type=jnp.float32)
        * score_scale
    )
    stacked_grad = (
        jnp.stack([queries_grad, keys_grad, values_grad], axis=2)
        .reshape(item_count, item_length, 3, local_width)
        .astype(jnp.bfloat16)
    )
    stacked_f = stacked_grad.astype(jnp.float32)
    input_bias_grad = jnp.stack(
        [jnp.sum(stacked_f[:, :, 0], axis=(0, 1)), jnp.sum(stacked_f[:, :, 2], axis=(0, 1))]
    )
    input_weight_grad = jnp.einsum(
        "bsd,bske->dke", hidden_one, stacked_grad, preferred_element_type=jnp.float32
    )
    hidden_one_part = jnp.einsum(
        "bske,dke->bsd", stacked_grad, input_weight, preferred_element_type=jnp.float32
    ).reshape(rows_all, model_width)
    hidden_one_grad = lax.psum(hidden_one_part, "tensor")
    gate_one_grad = jnp.sum(residual_grad * attention, axis=1)
    hidden_one_grad = hidden_one_grad.reshape(item_count, item_length, model_width)
    shift_one_grad = jnp.sum(hidden_one_grad, axis=1)
    scale_one_grad = jnp.sum(hidden_one_grad * normed_one, axis=1)
    tokens_grad = residual_grad + norm_back(
        hidden_one_grad * (1.0 + scale_one), normed_one, inverse_one
    )
    modulation_grad = jnp.stack(
        [
            shift_one_grad,
            scale_one_grad,
            gate_one_grad,
            shift_two_grad,
            scale_two_grad,
            gate_two_grad,
        ],
        axis=1,
    )
    column_start = lax.axis_index("tensor") * modulate_weight.shape[2]
    own_grad = lax.dynamic_slice_in_dim(modulation_grad, column_start, modulate_weight.shape[2], 2)
    modulate_weight_grad = jnp.einsum(
        "bd,bke->dke", silu_condition.astype(jnp.float32), own_grad, precision=HIGHEST
    )
    modulate_bias_grad = jnp.sum(own_grad, axis=0)
    gate_grad = jnp.stack([head_gate_grad, group_gate_grad], axis=-1)
    logit_grad = gate_grad * mask_rows * sigmoid_out * (1.0 - sigmoid_out)
    router_weight_grad = jnp.einsum(
        "bd,bhc->dhc", condition_low.astype(jnp.float32), logit_grad, precision=HIGHEST
    )
    router_bias_grad = jnp.sum(logit_grad, axis=0)
    summed = lax.psum(
        (
            modulate_weight_grad,
            modulate_bias_grad,
            input_weight_grad,
            input_bias_grad,
            output_weight_grad,
            output_bias_grad,
            expand_weight_grad,
            expand_bias_grad,
            reduce_weight_grad,
            reduce_bias_grad,
            router_weight_grad,
            router_bias_grad,
        ),
        "dp",
    )
    return (
        block_output.reshape(rows_all, model_width),
        tokens_grad.reshape(rows_all, model_width),
    ) + tuple(summed)


def solution(mesh):
    return jax.shard_map(
        body,
        mesh=mesh,
        in_specs=(
            P("dp", None),
            P("dp", None),
            P("dp"),
            P(None, "tensor", None),
            P(None, None, "tensor"),
            P(None, "tensor"),
            P(None, None, "tensor"),
            P(None, "tensor"),
            P("tensor", None),
            P(),
            P(None, "tensor"),
            P("tensor"),
            P("tensor", None),
            P(),
            P(None, "tensor", None),
            P("tensor", None),
            P("dp", None),
        ),
        out_specs=(
            P("dp", None),
            P("dp", None),
            P(None, None, "tensor"),
            P(None, "tensor"),
            P(None, None, "tensor"),
            P(None, "tensor"),
            P("tensor", None),
            P(),
            P(None, "tensor"),
            P("tensor"),
            P("tensor", None),
            P(),
            P(None, "tensor", None),
            P("tensor", None),
        ),
        check_vma=False,
    )
```

profile of v0, /device:TPU:0, one launch (start us, length us, event | category | flops | bytes accessed | tf_op | source)
XLA Modules:
  0.0 1133.5 jit_solution(17159783250025493048)
XLA Ops:
  15.8 28.7 %all_gather.3 = f32[8,6,1152]{1,0,2:T(8,128)} all-gather(f32[8,6,144]{1,0,2:T(8,128)S(1)} %copy.78), channel_id=1, replica_groups=mesh['dp'=4,'tensor'=8] {'tensor'}, dimensions={2}, use_global_device_ids=true | all-gather | bytes 248832 | tf_op jit(solution)/shard_map/all_gather | solution.py:73
  44.5 22.1 %fusion.64 = (f32[8,1,1152]{1,0,2:T(8,128)}, f32[8,1,1152]{1,0,2:T(8,128)}, f32[8,1,1152]{1,0,2:T(8,128)}, f32[8,1,1152]{1,0,2:T(8,128)}, f32[8,1,1152]{1,0,2:T(8,128)}, /*index=5*/f32[8,1,1152]{1,0,2:T(8,128)}) fusion(f32[8,6,1152]{1,0,2:T(8,128)} %all_gather.3), kind=kLoop, calls=%fused_computation.135 | loop fusion | bytes 442368 | tf_op jit(solution)/shard_map/slice | solution.py:75
  73.5 4.9 fusion.17
  84.3 5.3 fusion.70
  90.8 4.4 copy.121
  109.0 4.5 convert_reduce_fusion
  113.5 5.3 broadcast_multiply_fusion
  121.5 4.4 copy.122
  126.0 102.1 %all-reduce.8.cloned.1.call-done = f32[2048,1152]{1,0:T(8,128)} async-done(((f32[2048,1152]{1,0:T(8,128)}), f32[2048,1152]{1,0:T(8,128)}) %all-reduce.8.cloned.1.call-update) | async-done | bytes 9437200 | tf_op jit(solution)/shard_map/psum | solution.py:117
  228.0 10.4 fusion.62
  238.4 4.9 multiply_reduce_fusion.4
  248.0 8.9 multiply_convert_fusion
  258.3 6.8 fusion.72
  265.2 9.8 fusion.71
  275.0 128.3 %all-reduce.10.cloned.1.call-done = f32[2048,1152]{1,0:T(8,128)} async-done(((f32[2048,1152]{1,0:T(8,128)}), f32[2048,1152]{1,0:T(8,128)}) %all-reduce.10.cloned.1.call-update) | async-done | bytes 9437200 | tf_op jit(solution)/shard_map/psum | solution.py:154
  403.2 8.1 fusion.9
  412.4 10.7 convert_reduce_fusion.1
  434.1 5.4 convolution_bitcast_fusion
  440.2 7.9 fusion.75
  448.1 4.7 fusion.74
  452.9 4.3 fusion.73
  457.2 6.6 fusion.22
  463.8 215.9 %all-reduce.12.cloned.1.call-done = (f32[2048,1152]{1,0:T(8,128)}, f32[2048,1152]{1,0:T(8,128)}) async-done(((f32[2048,1152]{1,0:T(8,128)}, f32[2048,1152]{1,0:T(8,128)}), (f32[2048,1152]{1,0:T(8,128)}, f32[2048,1152]{1,0:T(8,128)})) %all-reduce.12.cloned.1.call-update) | async-done | bytes 18874384 | tf_op jit(solution)/shard_map/psum | solution.py:138
  679.7 22.3 %fusion.7 = (f32[8,1152]{1,0:T(8,128)S(1)}, f32[8,1152]{1,0:T(8,128)S(1)}, f32[8,1152]{1,0:T(8,128)S(1)}, f32[8,1152]{1,0:T(8,128)S(1)}, f32[8,1152]{1,0:T(8,128...) fusion(f32[2048,1152]{1,0:T(8,128)} %all-reduce.10.cloned.1.call-done, f32[2048,1152]{1,0:T(8,128)} %all-reduce.8.cloned.1.call-done, ...), kind=kLoop, calls=%fused_computation.17 | loop fusion | flops 61286400 | bytes 56976384 | tf_op jit(solution)/shard_map/reduce_sum | solution.py:158
  705.9 4.6 copy.123
  710.5 5.8 fusion.21
  718.7 6.9 fusion.8
  725.6 11.0 fusion.2
  736.6 11.9 %multiply_add_fusion = f32[2048,1152]{1,0:T(8,128)} fusion(f32[2048,1152]{1,0:T(8,128)} %get-tuple-element.52, f32[2048,1152]{1,0:T(8,128)} %get-tuple-element.31, bf16[2048,1152]{1,0:T(8,128)(2,1)} %param.17, f32[2048]{0:T(1024)S(1)} %broadcast_multiply_fusion.1, f32[2048]{0:T(1024)S(1)} %broadcast_multiply_fusion.2, f32[2048]{0:T(1024)S(1)} %copy-done.30, ...), kind=kLoop, calls=%fused_computation.24 | loop fusion | flops 21233664 | bytes 33099776 | tf_op jit(solution)/shard_map/add | solution.py:213
  748.7 26.9 %all-reduce.1 = (f32[6,144]{1,0:T(8,128)}, f32[2,144]{1,0:T(2,128)}, f32[1152]{0:T(1024)}, f32[576]{0:T(1024)}, f32[1152]{0:T(1024)}, /*index=5*/f32[1152,2,2]{0,2,1:T(2,128)}, f32[2,2]{1,0:T(2,128)}) all-reduce(f32[6,144]{1,0:T(8,128)S(1)} %dynamic-slice_reduce_fusion, ...), channel_id=1, replica_groups=mesh['dp'=4,'tensor'=8] {'dp'}, use_global_device_ids=true, to_apply=%region_23.24 | all-reduce | flops 8644 | bytes 69152 | tf_op jit(solution)/shard_map/psum | solution.py:239
  775.6 341.5 %all-reduce.14.cloned.1.call-done = (f32[1152,6,144]{0,2,1:T(8,128)}, f32[1152,3,144]{0,2,1:T(8,128)}, f32[144,1152]{1,0:T(8,128)}, f32[1152,576]{0,1:T(8,128)}, f32[576,1152]{1,0:T(8,128)}) async-done(((f32[1152,6,144]{0,2,1:T(8,128)}, f32[1152,3,144]{0,2,1:T(8,128)}, f32[144,1152]{1,0:T(8,128)}, f32[1152,576]{0,1:T(8,128)}, f32[576,1152]{1,0:T(8,128)}), (f32[1152,6,144]{0,2,1:T(8,128)}, ...) | async-done | bytes 11943952 | tf_op jit(solution)/shard_map/psum | solution.py:239
  1117.1 4.5 copy.141
  (211 shorter events, 68.8 us)
Async XLA Ops:
  7.2 7.6 copy-start
  7.2 7.0 copy-start.37
  7.2 7.6 copy-start.25
  7.2 220.8 %all-reduce.8.cloned.1.call-start = ((), (), s32[]{:S(2)}) async-start(), calls=%async_computation | async-start | bytes 18874368 | tf_op jit(solution)/shard_map/psum | solution.py:117
  10.4 34.1 %copy-start.27 = (f32[2048]{0:T(1024)}, f32[2048]{0:T(1024)S(1)}, u32[]{:S(2)}) copy-start(f32[2048]{0:T(1024)S(1)} %broadcast_multiply_fusion.6) | copy-start | bytes 24580
  66.7 6.8 copy-start.48
  84.3 5.4 copy-start.7
  89.7 313.6 %all-reduce.10.cloned.1.call-start = ((), (), s32[]{:S(2)}) async-start(), calls=%async_computation.1 | async-start | bytes 18874368 | tf_op jit(solution)/shard_map/psum | solution.py:154
  102.2 6.8 copy-start.23
  113.5 5.3 copy-start.11
  238.4 6.4 copy-start.2
  238.4 8.6 slice-start.2
  238.4 8.7 slice-start.4
  247.0 9.9 copy-start.13
  265.1 414.6 %all-reduce.12.cloned.1.call-start = ((), (), s32[]{:S(2)}) async-start(), calls=%async_computation.2 | async-start | bytes 37748736 | tf_op jit(solution)/shard_map/psum | solution.py:138
  403.2 9.1 copy-start.5
  412.4 10.7 copy-start.12
  439.5 8.6 slice-start
  439.5 677.6 %all-reduce.14.cloned.1.call-start = ((), (), s32[]{:S(2)}) async-start(), calls=%async_computation.3 | async-start | bytes 23887872 | tf_op jit(solution)/shard_map/psum | solution.py:239
  440.2 7.9 slice-start.1
  440.2 7.9 copy-start.54
  679.7 22.4 %copy-start.26 = (f32[8,1152]{1,0:T(8,128)S(1)}, f32[8,1152]{1,0:T(8,128)}, u32[]{:S(2)}) copy-start(f32[8,1152]{1,0:T(8,128)} %param.18) | copy-start | bytes 110596
  710.5 6.0 copy-start.32
  710.5 7.9 copy-start.43
  710.5 7.9 copy-start.44
  710.5 8.1 copy-start.28
  710.5 8.1 copy-start.30
  718.6 6.9 copy-start.24
  736.6 12.0 %copy-start.31 = (f32[1152]{0:T(1024)S(1)}, f32[1152]{0:T(1024)}, u32[]{:S(2)}) copy-start(f32[1152]{0:T(1024)} %get-tuple-element.46) | copy-start | bytes 13828
  736.6 12.0 %copy-start.40 = (f32[576]{0:T(1024)S(1)}, f32[576]{0:T(1024)}, u32[]{:S(2)}) copy-start(f32[576]{0:T(1024)} %get-tuple-element.58) | copy-start | bytes 6916
  1117.1 5.8 copy-start.22
  1117.1 6.6 copy-start.15
  (34 other events, 84.1 us)
Sparse Core Ops, SparseCore 0:
  89.8 138.2 all-reduce.7
  265.2 137.9 all-reduce.9
  439.6 240.0 all-reduce.11
  706.0 410.9 all-reduce.13
where the time goes:
time: 1140 us; the launch traced here: 1130 us
  waiting for transfers between devices  788 us (69%)
  other arithmetic  112 us (10%)
  matrix products  84.4 us (7%)
  local copies, waits for them, and re-layouts  78.2 us (7%)
  blocking collectives  55.6 us (5%)
  between operations  14.9 us (1%)
    psum x1, waiting for transfers between devices, body(): lax.psum((modulate_weight_grad, modulate_bias_grad, input_weight_grad, in...  341 us
    psum x1, waiting for transfers between devices, body(): lax.psum(mlp_part, 'tensor') + reduce_bias.astype(jnp.float32)  216 us
    psum x1, waiting for transfers between devices, body(): lax.psum(hidden_two_part, 'tensor')  128 us
    psum x1, waiting for transfers between devices, body(): lax.psum(attention_part, 'tensor') + output_bias.astype(jnp.float32)  102 us
    unnamed x144, local copies, waits for them, and re-layouts  51.5 us
    all_gather x1, blocking collectives, body(): modulation = lax.all_gather(modulate_part, 'tensor', axis=2, tiled=True)  28.7 us
    psum x1, blocking collectives, body(): lax.psum((modulate_weight_grad, modulate_bias_grad, input_weight_grad, in...  26.9 us
  transfers between devices with their start and end apart: 4, of which 4 were waited for; matrix products, arithmetic and copies ran while one was open for 10% of the time, Pallas kernels for 0%

commit v1 on v0

v1 whole, which is shorter than its diff:
```python
import functools
import math

import jax
import jax.numpy as jnp
from jax import lax
from jax.experimental import pallas as pl
from jax.experimental.pallas import tpu as pltpu
from jax.sharding import PartitionSpec as P

BF = jnp.bfloat16
F32 = jnp.float32
MESH = pl.DeviceIdType.MESH
EPSILON = 1e-06
GELU_A = math.sqrt(2.0 / math.pi)
GELU_B = 0.044715
VMEM_LIMIT = 58 << 20


def nt(left, right):
    return lax.dot_general(left, right, (((1,), (1,)), ((), ())), preferred_element_type=F32)


def nn(left, right):
    return lax.dot_general(left, right, (((1,), (0,)), ((), ())), preferred_element_type=F32)


def tn(left, right):
    return lax.dot_general(left, right, (((0,), (0,)), ((), ())), preferred_element_type=F32)


def flip(value, mask, bits):
    total = 0
    for bit in range(bits):
        unit = 1 << bit
        total = total + lax.rem(value // unit + mask // unit, 2) * unit
    return total


def norm(values):
    center = values - jnp.mean(values, axis=-1, keepdims=True)
    inverse = lax.rsqrt(jnp.mean(center * center, axis=-1, keepdims=True) + EPSILON)
    return center * inverse, inverse


def norm_back(grad, normed, inverse):
    mean_grad = jnp.mean(grad, axis=-1, keepdims=True)
    mean_cross = jnp.mean(grad * normed, axis=-1, keepdims=True)
    return inverse * (grad - mean_grad - normed * mean_cross)


class Plan:
    def __init__(self, groups, members, rows, items, width, heads, modwidth, headwidth, channels):
        self.D = groups
        self.T = members
        self.G = members // 2
        self.bits = self.G.bit_length() - 1
        self.tbits = members.bit_length() - 1
        self.dbits = groups.bit_length() - 1
        self.R = rows
        self.I = items
        self.L = rows // items
        self.W = width
        self.Rc = rows // 2
        self.Ro = rows // members
        self.Ic = items // 2
        self.sub = self.L // self.Ro
        self.lh = heads
        self.mw = modwidth
        self.cw = -(-modwidth // 128) * 128
        self.hw = headwidth
        self.hd = headwidth // heads
        self.ch = channels
        self.gc = channels // heads
        self.hr = 2 * headwidth
        self.halvings = min(self.dbits, 2)
        self.flips = [1, 3][: self.dbits] + [1 << b for b in range(2, self.dbits)]
        self.units = 1 << self.halvings
        self.zr = 4 * self.hw // (2 * self.units)

    def place(self):
        d = lax.axis_index("dp")
        t = lax.axis_index("tensor")
        return d, t, t // 2, lax.rem(t, 2)


def meet(devices):
    barrier = pltpu.get_barrier_semaphore()
    for device in devices:
        pl.semaphore_signal(barrier, inc=1, device_id=device, device_id_type=MESH)
    pl.semaphore_wait(barrier, len(devices))


def remote(src, dst, send, recv, device):
    return pltpu.make_async_remote_copy(
        src_ref=src, dst_ref=dst, send_sem=send, recv_sem=recv, device_id=device, device_id_type=MESH
    )


class GroupSum:
    def __init__(self, g, work, inbox, full, send, recv, device):
        self.g, self.work, self.inbox, self.full = g, work, inbox, full
        self.send, self.recv, self.device = send, recv, device
        d = lax.axis_index("dp")
        low, high = lax.rem(d, 2), lax.rem(d // 2, 2)
        both = low + high - 2 * low * high
        self.steps = g.dbits
        self.flips = [g.flips, g.flips[1::-1] + g.flips[2:]]
        keeps = [[low], [low]] if g.dbits == 1 else [[both, high], [high, low]]
        self.places = []
        for which in range(2):
            start, size, rows = which * g.units, g.units, []
            for step in range(self.steps):
                if step < g.halvings:
                    half = size // 2
                    keep = start + keeps[which][step] * half
                    away = start + (1 - keeps[which][step]) * half
                    rows.append((keep, away, half))
                    start, size = keep, half
                else:
                    rows.append((start, start, size))
            self.places.append(rows)

    def peer(self, which, step):
        return self.device(self.flips[which][step])

    def box(self, which, step):
        g = self.g
        base = sum(g.units >> (s + 1) if s < g.halvings else 1 for s in range(step))
        size = self.places[which][step][2]
        return self.inbox.at[which, pl.ds(base, size)]

    def copy(self, which, step):
        _, away, size = self.places[which][step]
        return remote(
            self.work.at[pl.ds(away, size)], self.box(which, step), self.send.at[which, step],
            self.recv.at[which, step], self.peer(which, step),
        )

    def start(self, step):
        for which in range(2):
            self.copy(which, step).start()

    def add(self, step):
        for which in range(2):
            keep, _, size = self.places[which][step]
            copy = self.copy(which, step)
            if step < self.g.halvings:
                copy.wait_recv()
            else:
                copy.wait()
            rows = pl.ds(keep, size)
            self.work[rows] = (self.work[rows].astype(F32) + self.box(which, step)[...].astype(F32)).astype(BF)

    def sent(self):
        for step in range(self.g.halvings):
            for which in range(2):
                self.copy(which, step).wait_send()

    def spread(self, which, step):
        keep, _, size = self.places[which][step]
        rows = self.full.at[pl.ds(keep, size)]
        slot = self.steps + step
        return remote(rows, rows, self.send.at[which, slot], self.recv.at[which, slot], self.peer(which, step))

    def gathered(self, which, step):
        _, away, size = self.places[which][step]
        rows = self.full.at[pl.ds(away, size)]
        slot = self.steps + step
        return remote(rows, rows, self.send.at[which, slot], self.recv.at[which, slot], self.peer(which, step))

    def spread_start(self, step):
        for which in range(2):
            if step == self.g.halvings - 1:
                keep, _, size = self.places[which][step]
                self.full[pl.ds(keep, size)] = self.work[pl.ds(keep, size)]
            self.spread(which, step).start()

    def spread_wait(self, step):
        for which in range(2):
            self.spread(which, step).wait_send()
            self.gathered(which, step).wait_recv()

    @staticmethod
    def scratch(g, rows):
        boxes = sum(g.units >> (s + 1) if s < g.halvings else 1 for s in range(g.dbits))
        dma = pltpu.SemaphoreType.DMA
        return [
            pltpu.VMEM((2 * g.units, rows, g.W), BF), pltpu.VMEM((2, boxes, rows, g.W), BF),
            dma((2, 2 * g.dbits)), dma((2, 2 * g.dbits)),
        ]


def call(kernel, name, inputs, in_spaces, outs, out_spaces, scratch, collective, cost=None):
    spec = {
        "v": pl.BlockSpec(memory_space=pltpu.VMEM),
        "h": pl.BlockSpec(memory_space=pl.ANY),
        "s": pl.BlockSpec(memory_space=pltpu.SMEM),
    }
    flops, moved = cost or (10**8, 10**7)
    return pl.pallas_call(
        kernel,
        name=name,
        out_shape=[jax.ShapeDtypeStruct(s, t) for s, t in outs],
        in_specs=[spec[x] for x in in_spaces],
        out_specs=[spec[x] for x in out_spaces],
        scratch_shapes=scratch,
        cost_estimate=pl.CostEstimate(flops=flops, bytes_accessed=moved, transcendentals=0),
        compiler_params=pltpu.CompilerParams(
            collective_id=collective, has_side_effects=collective is not None, vmem_limit_bytes=VMEM_LIMIT
        ),
    )(*inputs)


def start_kernel(
    g, cond, wm, mb, ts, masks, rw, rb, eb, ib, wi, we, wr,
    mod, gat, dsg, smc, call_all, wix, wex, wrx,
    mpart, gx, sx, cx, send_m, recv_m, send_w, recv_w, send_c, recv_c,
):
    d, t, p, c = g.place()
    partner = (d, p * 2 + 1 - c)
    meet(
        [(d, flip(t, k, g.tbits)) for k in range(1, g.T)] + [(flip(d, k, g.dbits), t) for k in range(1, g.D)]
    )
    pair = [
        remote(src, dst, send_w.at[index], recv_w.at[index], partner)
        for index, (src, dst) in enumerate(((wi, wix), (we, wex), (wr, wrx)))
    ]
    for copy in pair:
        copy.start()
    value = cond[...]
    silu = (value / (1.0 + jnp.exp(-value))).astype(BF)
    part = nt(silu, wm[...])
    w = g.mw
    bias = mb[...].astype(F32)
    for row in range(6):
        mpart[t, :, row * w : (row + 1) * w] = part[:, row * w : (row + 1) * w] + bias[row : row + 1]

    def spread(k):
        return remote(
            mpart.at[t], mpart.at[t], send_m.at[k], recv_m.at[k], (d, flip(t, k, g.tbits))
        )

    for k in range(1, g.T):
        spread(k).start()
    low = value.astype(BF)
    steps = masks.shape[2]
    row = lax.broadcasted_iota(jnp.int32, (g.I, steps), 0)
    wanted = jnp.zeros((g.I, steps), jnp.int32)
    for item in range(g.I):
        wanted = jnp.where(row == item, ts[item], wanted)
    hot = (wanted == lax.broadcasted_iota(jnp.int32, (g.I, steps), 1)).astype(F32).astype(BF)
    dsg[...] = jnp.zeros_like(dsg)
    gx[0] = jnp.zeros((g.I, 128), F32)
    scale = rb[...].astype(F32)
    for h in range(g.lh):
        logits = nt(low, rw[h]) + scale[h : h + 1]
        sigmoid = 1.0 / (1.0 + jnp.exp(-logits))
        mask = nt(hot, masks[h].astype(F32).astype(BF))
        dsg[:, 2 * h : 2 * h + 2] = mask * sigmoid * (1.0 - sigmoid)
        gx[0, :, 2 * h : 2 * h + 2] = mask * sigmoid
    sx[0] = jnp.zeros((8, g.W), F32)
    sx[0, 0:1, : g.ch] = eb[...]
    sx[0, 1:3, : g.hw] = ib[...].astype(F32)
    small = [
        remote(gx.at[0], gx.at[1], send_w.at[3], recv_w.at[3], partner),
        remote(sx.at[0], sx.at[1], send_w.at[4], recv_w.at[4], partner),
    ]
    for copy in small:
        copy.start()

    def conditions(k):
        return remote(cond, cx.at[d], send_c.at[k], recv_c.at[k], (flip(d, k, g.dbits), t))

    for k in range(1, g.D):
        conditions(k).start()
    cx[d] = value
    for k in range(1, g.T):
        spread(k).wait()
    for member in range(g.T):
        for row in range(6):
            mod[row, :, member * w : (member + 1) * w] = mpart[member, :, row * w : (row + 1) * w]
    for copy in small:
        copy.wait()
    gat[...] = gx[...]
    smc[...] = sx[...]
    for copy in pair:
        copy.wait()
    for k in range(1, g.D):
        conditions(k).wait()
    call_all[...] = cx[...]


def split_heads(g, wide):
    return [wide[r * g.hw + h * g.hd : r * g.hw + (h + 1) * g.hd] for r in range(3) for h in range(g.lh)]


def attend_kernel(
    g, tokens, mod, gat, smc, wi, wix, wo, ob,
    h1, qkv, lse, att, res, h2, gath, wof,
    tok, gsend, gbuf, wob, load, keep, send, recv, send_o, recv_o, send_f, recv_f,
):
    d, t, p, c = g.place()
    partner = (d, p * 2 + 1 - c)
    weights = (wi, wix)
    meet([(d, flip(p, k, g.bits) * 2 + c) for k in range(1, g.G)] + [partner])

    def share(k):
        return remote(wo, wob.at[t], send_o.at[k], recv_o.at[k], (d, flip(p, k, g.bits) * 2 + c))

    def forward(k):
        row = flip(p, k, g.bits) * 2 + c
        src = wo if k == 0 else wob.at[row]
        return remote(src, wob.at[row], send_f.at[k], recv_f.at[k], partner)

    for k in range(1, g.G):
        share(k).start()
    forward(0).start()
    wob[t] = wo[...]
    copy = pltpu.make_async_copy(tokens.at[pl.ds(pl.multiple_of(c * g.Rc, g.Rc), g.Rc)], tok, load)
    copy.start()
    copy.wait()
    scale = 1.0 / math.sqrt(g.hd)
    ones = jnp.ones((8, g.L), BF)

    def chunk(j):
        i, u = j // g.sub, lax.rem(j, g.sub)
        src = gsend.at[i] if g.sub == 1 else gsend.at[i, :, :, pl.ds(pl.multiple_of(u * g.Ro, g.Ro), g.Ro)]
        return src, gbuf.at[pl.ds(p * 2, 2)]

    def away(j):
        src, dst = chunk(j)
        return remote(src, dst, send.at[j], recv.at[p], (d, j * 2 + c))

    def arrive(j):
        src, _ = chunk(j)
        dst = gbuf.at[pl.ds(j * 2, 2)]
        return remote(src, dst, send.at[j], recv.at[j], (d, j * 2 + c))

    def home():
        src, dst = chunk(p)
        return pltpu.make_async_copy(src, dst, keep)

    def item(ii, carry):
        i = flip(p // g.sub, g.Ic - 1 - ii, g.bits)
        rows = pl.ds(pl.multiple_of(i * g.L, g.L), g.L)
        row = c * g.Ic + i
        normed, _ = norm(tok[rows].astype(F32))
        hidden = (
            normed * (1.0 + mod[1, pl.ds(row, 1), :]) + mod[0, pl.ds(row, 1), :]
        ).astype(BF)
        h1[rows] = hidden
        for s in range(2):
            wide = nt(weights[s][...], hidden)
            core = c + s - 2 * c * s
            parts = split_heads(g, wide)
            rowsum = smc[s].astype(BF)
            bias = []
            for r in (1, 2):
                line = jnp.where(lax.broadcasted_iota(jnp.int32, (8, g.hw), 0) == r, rowsum[:, : g.hw].astype(F32), 0.0)
                bias.append(tn(line.astype(BF), ones))
            for h in range(g.lh):
                hh = s * g.lh + h
                rows_h = slice(h * g.hd, (h + 1) * g.hd)
                q = (parts[h] + bias[0][rows_h]).astype(BF)
                k = parts[g.lh + h].astype(BF)
                v = (parts[2 * g.lh + h] + bias[1][rows_h]).astype(BF)
                qkv[hh * 3 + 0, :, rows] = q
                qkv[hh * 3 + 1, :, rows] = k
                qkv[hh * 3 + 2, :, rows] = v
                scores = tn(k, q) * scale
                peak = jnp.max(scores, axis=0, keepdims=True)
                powers = jnp.exp(scores - peak)
                total = jnp.sum(powers, axis=0, keepdims=True)
                lse[hh : hh + 1, rows] = peak + jnp.log(total)
                probs = (powers * (1.0 / total)).astype(BF)
                mixed = nn(v, probs)
                gate = gat[s, pl.ds(row, 1), 2 * h : 2 * h + 1]
                gsend[i, core, rows_h, :] = (mixed * gate).astype(BF)
        for u in range(g.sub):
            j = i * g.sub + u

            @pl.when(j == p)
            def _():
                home().start()

            @pl.when(j != p)
            def _():
                away(j).start()

        return carry

    lax.fori_loop(0, g.Ic, item, 0)
    home().wait()
    for k in range(1, g.G):
        arrive(flip(p, k, g.bits)).wait_recv()
    heads = gbuf[...].reshape(g.T * g.hw, g.Ro)
    gath[...] = heads
    for k in range(1, g.G):
        share(k).wait_recv()
        forward(k).start()
    for k in range(g.G):
        forward(k).wait_recv()
    full = wob[...].reshape(g.T * g.hw, g.W)
    wof[...] = full
    attention = tn(heads, full) + ob[...]
    own = c * g.Ic + p // g.sub
    base = tok[pl.ds(pl.multiple_of(p * g.Ro, g.Ro), g.Ro)].astype(F32)
    residual = base + mod[2, pl.ds(own, 1), :] * attention
    att[...] = attention
    res[...] = residual
    normed, _ = norm(residual)
    h2[...] = (normed * (1.0 + mod[4, pl.ds(own, 1), :]) + mod[3, pl.ds(own, 1), :]).astype(BF)
    for k in range(1, g.G):
        away(flip(p, k, g.bits)).wait_send()
        share(k).wait_send()
    for k in range(g.G):
        forward(k).wait_send()


def feed_kernel(
    g, h2, cotangent, mod, gat, smc, we_in, wex_in, wr_in, wrx_in,
    grad_out, mpart, dwf, small, gates, ebs,
    cot, we, wex, wr, wrx, h2buf, bgbuf, gch, egb, sgb, rgb, own_g, xs, xr,
    load, send_h, recv_h, send_g, recv_g, send_p, recv_p,
):
    d, t, p, c = g.place()
    partner = (d, p * 2 + 1 - c)
    wec = (we, wex)
    wrc = (wr, wrx)

    def chip(k):
        return (d, flip(p, k, g.bits) * 2 + c)

    cot_rows = cotangent.at[pl.ds(pl.multiple_of(c * g.Rc, g.Rc), g.Rc)]
    loads = [
        pltpu.make_async_copy(src, dst, load.at[index])
        for index, (src, dst) in enumerate(
            ((cot_rows, cot), (wr_in, wr), (wrx_in, wrx), (we_in, we), (wex_in, wex))
        )
    ]
    for copy in loads:
        copy.start()
    meet([chip(k) for k in range(1, g.G)] + [partner])

    def spread(k):
        return remote(h2, h2buf.at[k], send_h.at[k], recv_h.at[k], chip(k))

    for k in range(1, g.G):
        spread(k).start()
    h2buf[0] = h2[...]
    for copy in loads:
        copy.wait()
    lane = lax.broadcasted_iota(jnp.int32, (1, g.ch), 1)
    tile_row = lax.broadcasted_iota(jnp.int32, (8, 128), 0)
    tile_lane = lax.broadcasted_iota(jnp.int32, (8, 128), 1)
    ebs[...] = jnp.zeros_like(ebs)
    gates[...] = jnp.zeros_like(gates)

    def back(k):
        return remote(sgb.at[k - 1], rgb.at[k - 1], send_g.at[k], recv_g.at[k], chip(k))

    def block(k, carry):
        j = flip(p, k, g.bits)
        local = j // g.sub
        item = c * g.Ic + local
        rows = pl.ds(pl.multiple_of(j * g.Ro, g.Ro), g.Ro)
        here = pl.ds(pl.multiple_of(k * g.Ro, g.Ro), g.Ro)
        branch = (mod[5, pl.ds(item, 1), :] * cot[rows].astype(F32)).astype(BF)
        bgbuf[here] = branch
        grads = [nt(branch, wrc[s][...]) for s in range(2)]

        @pl.when(k > 0)
        def _():
            spread(k).wait_recv()

        hidden = h2buf[k]
        total = None
        for s in range(2):
            wide = nt(hidden, wec[s][...]) + smc[s, 0:1, : g.ch]
            inner = GELU_A * (wide + GELU_B * wide * wide * wide)
            tanh = jnp.tanh(inner)
            act = 0.5 * wide * (1.0 + tanh)
            slope = 0.5 * (1.0 + tanh) + 0.5 * wide * (1.0 - tanh * tanh) * (
                GELU_A * (1.0 + 3.0 * GELU_B * wide * wide)
            )
            gate = gat[s, pl.ds(item, 1), 1:2]
            for h in range(1, g.lh):
                gate = jnp.where(lane >= h * g.gc, gat[s, pl.ds(item, 1), 2 * h + 1 : 2 * h + 2], gate)
            gch[s, here] = (act * gate).astype(BF)
            line = jnp.sum(grads[s] * act, axis=0, keepdims=True)
            tile = gates[s]
            for h in range(g.lh):
                inside = jnp.where((lane >= h * g.gc) & (lane < (h + 1) * g.gc), line, 0.0)
                value = jnp.sum(inside, axis=1, keepdims=True)
                tile = tile + jnp.where((tile_row == local) & (tile_lane == 2 * h + 1), value, 0.0)
            gates[s] = tile
            egrad = (grads[s] * gate * slope).astype(BF)
            egb[s, here] = egrad
            ebs[s, 0:1, : g.ch] += jnp.sum(egrad.astype(F32), axis=0, keepdims=True)
            part = nn(egrad, wec[s][...])
            total = part if total is None else total + part

        @pl.when(k > 0)
        def _():
            sgb[k - 1] = total.astype(BF)
            back(k).start()

        @pl.when(k == 0)
        def _():
            own_g[...] = total

        return carry

    lax.fori_loop(0, g.G, block, 0)
    xs[0] = tn(gch[1], bgbuf[...]).astype(BF)

    def swap(index):
        return remote(xs.at[index], xr.at[index], send_p.at[index], recv_p.at[index], partner)

    swap(0).start()
    xs[1] = tn(egb[1], h2buf[...].reshape(g.Rc, g.W)).astype(BF)
    swap(1).start()
    unit = g.ch // g.units
    for index, (left, right) in enumerate(
        ((gch[0], bgbuf[...]), (egb[0], h2buf[...].reshape(g.Rc, g.W)))
    ):
        value = tn(left, right)
        swap(index).wait_recv()
        value = (value + xr[index].astype(F32)).astype(BF)
        for u in range(g.units):
            dwf[index * g.units + u] = value[u * unit : (u + 1) * unit]
    for k in range(g.G):
        rows = pl.ds(k * g.Ro, g.Ro)
        mpart[k] = (nn(gch[0, rows], wr[...]) + nn(gch[1, rows], wrx[...])).astype(BF)
    small[...] = jnp.zeros_like(small)
    small[7:8, :] = jnp.sum(bgbuf[0 : g.Ro].astype(F32), axis=0, keepdims=True)
    grad = own_g[...]
    for k in range(1, g.G):
        back(k).wait_recv()
        grad = grad + rgb[k - 1].astype(F32)
    grad_out[...] = grad
    for k in range(1, g.G):
        spread(k).wait_send()
        back(k).wait_send()
    swap(0).wait_send()
    swap(1).wait_send()


def unattend_kernel(
    g, hgrad, h1, qkv, lse, gat, wi, wix, small_in, mpart, dwf, mod, att, res, wof, gath, cotangent, rbias, ebs,
    gates_in,
    grad, rgrad, bout, dwz, dwf_out, lines, sums, pay, gates,
    hgs, hgbuf, wof_x, orr, osum, small, dqkv, acc, own_g, sgb, rgb, rmb, xs, xr, orv, sx, cot,
    work, inbox, send_z, recv_z,
    send_g, recv_g, send_m, recv_m, send_o, recv_o, send_s, recv_s, send_p, recv_p, send_a, recv_a, send_x, recv_x,
    load,
):
    d, t, p, c = g.place()
    partner = (d, p * 2 + 1 - c)
    weights = (wi, wix)
    block = c * g.G + p

    def chip(k):
        return (d, flip(p, k, g.bits) * 2 + c)

    def peer(k):
        return (d, flip(t, k, g.tbits))

    def group(k):
        return (flip(d, k, g.dbits), t)

    fetch = pltpu.make_async_copy(
        cotangent.at[pl.ds(pl.multiple_of(block * g.Ro, g.Ro), g.Ro)], cot, load.at[0]
    )
    fetch.start()
    half = pltpu.make_async_copy(dwf, work, load.at[1])
    half.start()
    first = pltpu.make_async_copy(mpart.at[0], rmb.at[0], load.at[2])
    first.start()
    meet([peer(k) for k in range(1, g.T)] + [group(k) for k in g.flips])

    def rest(k):
        return remote(osum.at[flip(p, k, g.bits)], orv.at[k - 1], send_o.at[k], recv_o.at[k], chip(k))

    def on(k):
        return remote(mpart.at[k], rmb.at[k], send_m.at[k], recv_m.at[k], chip(k))

    def sumup(k):
        return remote(small, sx.at[k], send_s.at[k], recv_s.at[k], peer(k))

    def heads_out(k):
        return remote(hgs.at[pl.ds(flip(p, k, g.bits) * 2, 2)], hgbuf.at[k], send_a.at[k], recv_a.at[k], chip(k))

    def cross(q):
        return remote(wof_x.at[2 * q + 1 - c], orr.at[q], send_x.at[q], recv_x.at[q], partner)

    half.wait()
    zsum = GroupSum(g, work, inbox, dwf_out, send_z, recv_z, group)
    zsum.start(0)
    fetch.wait()
    value = hgrad[...]
    own = c * g.Ic + p // g.sub
    normed, inverse = norm(res[...])
    cot_own = cot[...].astype(F32)
    residual = cot_own + norm_back(value * (1.0 + mod[4, pl.ds(own, 1), :]), normed, inverse)
    branch_one = (mod[2, pl.ds(own, 1), :] * residual).astype(BF)
    hgs[...] = nt(wof[...], branch_one).astype(BF).reshape(g.T, g.hw, g.Ro)
    for k in range(1, g.G):
        heads_out(k).start()
    hgbuf[0] = hgs[pl.ds(p * 2, 2)]
    for k in range(1, g.G):
        on(k).start()
    rgrad[...] = residual
    small[...] = small_in[...]
    small[2:3, :] = jnp.sum(residual * att[...], axis=0, keepdims=True)
    small[3:4, :] = jnp.sum(value, axis=0, keepdims=True)
    small[4:5, :] = jnp.sum(value * normed, axis=0, keepdims=True)
    small[6:7, :] = jnp.sum(branch_one.astype(F32), axis=0, keepdims=True)
    for k in range(1, g.T):
        sumup(k).start()
    wof_x[...] = nn(gath[...], branch_one).astype(BF).reshape(g.T, g.hw, g.W)
    for q in range(g.G):
        cross(q).start()
    scale = 1.0 / math.sqrt(g.hd)
    acc[...] = jnp.zeros_like(acc)
    ones = jnp.ones((8, g.L), BF)
    tile_row = lax.broadcasted_iota(jnp.int32, (8, 128), 0)
    tile_lane = lax.broadcasted_iota(jnp.int32, (8, 128), 1)
    gates[...] = gates_in[...]
    pay[...] = ebs[...]

    def back(k):
        return remote(sgb.at[k - 1], rgb.at[k - 1], send_g.at[k], recv_g.at[k], chip(k))

    def item(ii, carry):
        i = flip(p // g.sub, ii, g.bits)
        row = c * g.Ic + i
        rows = pl.ds(pl.multiple_of(i * g.L, g.L), g.L)
        slots = [ii * g.sub + (flip(lax.rem(p, g.sub), u, 4) if g.sub > 1 else 0) for u in range(g.sub)]
        hidden = h1[rows]
        total = None
        for u, slot in enumerate(slots):

            @pl.when(slot != 0)
            def _():
                heads_out(slot).wait_recv()

        @pl.when(ii == 1)
        def _():
            for q in range(g.G):
                cross(q).wait()
                osum[q] = (wof_x[2 * q + c].astype(F32) + orr[q].astype(F32)).astype(BF)
            for k in range(1, g.G):
                rest(k).start()

        @pl.when(ii == g.Ic - 1)
        def _():
            zsum.add(0)
            if g.dbits > 1:
                zsum.start(1)

        for s in range(2):
            core = c + s - 2 * c * s
            tile = gates[s]
            for h in range(g.lh):
                hh = s * g.lh + h
                q = qkv[hh * 3 + 0, :, rows]
                k = qkv[hh * 3 + 1, :, rows]
                v = qkv[hh * 3 + 2, :, rows]
                pieces = [hgbuf[slot, core, h * g.hd : (h + 1) * g.hd, :] for slot in slots]
                heads = (pieces[0] if g.sub == 1 else jnp.concatenate(pieces, axis=1)).astype(F32)
                probs = jnp.exp(tn(k, q) * scale - lse[hh : hh + 1, rows])
                low = probs.astype(BF)
                mixed = nn(v, low)
                value = jnp.sum(jnp.sum(heads * mixed, axis=0, keepdims=True), axis=1, keepdims=True)
                tile = tile + jnp.where((tile_row == i) & (tile_lane == 2 * h), value, 0.0)
                mixed_grad = (gat[s, pl.ds(row, 1), 2 * h : 2 * h + 1] * heads).astype(BF)
                probs_grad = tn(v, mixed_grad)
                values_grad = nt(mixed_grad, low)
                score = (
                    probs * (probs_grad - jnp.sum(probs_grad * probs, axis=0, keepdims=True))
                ).astype(BF)
                queries_grad = nn(k, score) * scale
                keys_grad = nt(q, score) * scale
                for r, value in enumerate((queries_grad, keys_grad, values_grad)):
                    dqkv[s, r * g.hw + h * g.hd : r * g.hw + (h + 1) * g.hd, :] = value.astype(BF)
            gates[s] = tile
            wide = dqkv[s]
            part = tn(wide, weights[s][...])
            total = part if total is None else total + part
            acc[s] += nn(wide, hidden)
            pay[s, 1:2, : 3 * g.hw] += nt(ones, wide)[0:1]
        for u, slot in enumerate(slots):
            piece = total[u * g.Ro : (u + 1) * g.Ro]

            @pl.when(slot == 0)
            def _():
                own_g[...] = piece

            @pl.when(slot != 0)
            def _():
                sgb[slot - 1] = piece.astype(BF)
                back(slot).start()

        return carry

    lax.fori_loop(0, g.Ic, item, 0)
    xs[...] = acc[1].astype(BF)
    swap = remote(xs, xr, send_p, recv_p, partner)
    swap.start()
    for step in range(1, g.dbits):
        zsum.add(step)
        if step + 1 < g.dbits:
            zsum.start(step + 1)
    zsum.spread_start(g.halvings - 1)
    value = small[...]
    for k in range(1, g.T):
        sumup(k).wait()
        value = value + sx[k]
    sums[...] = value
    out = osum[p].astype(F32)
    for k in range(1, g.G):
        rest(k).wait()
        out = out + orv[k - 1].astype(F32)
    swap.wait()
    for u in range(2 * g.units):
        low = u * g.zr
        if low < 3 * g.hw:
            span = slice(low, low + g.zr)
            dwz[u] = (acc[0, span] + xr[span].astype(F32)).astype(BF)
        else:
            dwz[u] = out[low - 3 * g.hw : low - 3 * g.hw + g.zr].astype(BF)
    for step in reversed(range(g.halvings - 1)):
        zsum.spread_wait(step + 1)
        zsum.spread_start(step)
    first.wait()
    branch = rmb[0].astype(F32)
    for k in range(1, g.G):
        on(k).wait()
        branch = branch + rmb[k].astype(F32)
    branch = branch + rbias[...]
    bout[...] = (res[...] + mod[5, pl.ds(own, 1), :] * branch).astype(BF)
    lines[...] = small[...]
    lines[5:6, :] = jnp.sum(cot[...].astype(F32) * branch, axis=0, keepdims=True)
    value = own_g[...]
    for k in range(1, g.G):
        back(k).wait()
        value = value + rgb[k - 1].astype(F32)
    grad[...] = value
    zsum.spread_wait(0)
    zsum.sent()
    for k in range(1, g.G):
        heads_out(k).wait_send()


def finish_kernel(
    g, grad, rgrad, tokens, mod, lines_in, sums, bout, pay, gates, dsg, dwz,
    tall, ball, colall, zall, logall, dwz_out,
    tok, tsend, stage, cbuf, zbuf, lbuf, pbuf, gbuf, work, inbox, send_z, recv_z,
    load, send_t, recv_t, send_f, recv_f, send_c, recv_c, send_p, recv_p, send_s, recv_s, keep,
):
    d, t, p, c = g.place()
    partner = (d, p * 2 + 1 - c)

    def chip(k):
        return (d, flip(p, k, g.bits) * 2 + c)

    def peer(k):
        return (d, flip(t, k, g.tbits))

    def group(k):
        return (flip(d, k, g.dbits), t)

    meet([peer(k) for k in range(1, g.T)] + [group(k) for k in range(1, g.D)])
    block = c * g.G + p
    mine = pl.ds(pl.multiple_of(block * g.Ro, g.Ro), g.Ro)
    copy = pltpu.make_async_copy(tokens.at[mine], tok, load)
    copy.start()
    swaps = [
        remote(pay.at[1], pbuf, send_p.at[0], recv_p.at[0], partner),
        remote(gates.at[1], gbuf, send_p.at[1], recv_p.at[1], partner),
    ]
    for swap in swaps:
        swap.start()
    zsum = GroupSum(g, work, inbox, dwz_out, send_z, recv_z, group)
    work[...] = dwz[...]
    zsum.start(0)

    def spread(which, src, dst, k):
        return remote(src, dst.at[mine], send_t.at[which, k], recv_t.at[which, k], chip(k))

    for k in range(1, g.G):
        spread(0, bout, ball, k).start()
    copy.wait()
    own = c * g.Ic + p // g.sub
    normed, inverse = norm(tok[...].astype(F32))
    value = grad[...]
    scaled = value * (1.0 + mod[1, pl.ds(own, 1), :])
    tsend[...] = (rgrad[...] + norm_back(scaled, normed, inverse)).astype(BF)
    lines = lines_in[...]
    kind = lax.broadcasted_iota(jnp.int32, lines.shape, 0)
    first = jnp.sum(value, axis=0, keepdims=True)
    second = jnp.sum(value * normed, axis=0, keepdims=True)
    lines = jnp.where(kind == 0, first, jnp.where(kind == 1, second, lines))
    w = g.mw
    stage[...] = jnp.zeros_like(stage)
    for member in range(g.T):
        stage[member, :, :w] = lines[:, member * w : (member + 1) * w]

    def columns(k):
        return remote(stage.at[flip(t, k, g.tbits)], cbuf.at[d, t], send_c.at[k], recv_c.at[k], peer(k))

    def column_in(k):
        return remote(stage.at[t], cbuf.at[d, flip(t, k, g.tbits)], send_c.at[k], recv_c.at[k], peer(k))

    for k in range(1, g.T):
        columns(k).start()
    cbuf[d, t] = stage[t]
    for k in range(1, g.G):
        spread(1, tsend, tall, k).start()
    local = [
        pltpu.make_async_copy(bout, ball.at[mine], keep.at[0]),
        pltpu.make_async_copy(tsend, tall.at[mine], keep.at[1]),
    ]
    for item in local:
        item.start()

    def forward(which, dst, k):
        rows = pl.ds(pl.multiple_of((c * g.G + flip(p, k, g.bits)) * g.Ro, g.Ro), g.Ro)
        return remote(dst.at[rows], dst.at[rows], send_f.at[which, k], recv_f.at[which, k], partner)

    def arrive(which, dst, k):
        rows = pl.ds(pl.multiple_of((c * g.G + flip(p, k, g.bits)) * g.Ro, g.Ro), g.Ro)
        return remote(bout, dst.at[rows], send_t.at[which, k], recv_t.at[which, k], chip(k))

    def arrive_forward(which, dst, k):
        rows = pl.ds(pl.multiple_of(((1 - c) * g.G + flip(p, k, g.bits)) * g.Ro, g.Ro), g.Ro)
        return remote(dst.at[rows], dst.at[rows], send_f.at[which, k], recv_f.at[which, k], partner)

    for step in range(g.dbits):
        zsum.add(step)
        if step + 1 < g.dbits:
            zsum.start(step + 1)
    zsum.spread_start(g.halvings - 1)
    for swap in swaps:
        swap.wait()
    zbuf[d] = jnp.zeros((8, g.W), F32)
    zbuf[d, 0:2] = pay[0, 0:2] + pbuf[0:2]
    zbuf[d, 2:4] = sums[6:8]
    both = jnp.concatenate([gates[0, : g.Ic], gbuf[: g.Ic]], axis=0)
    turned = jnp.concatenate([gbuf[: g.Ic], gates[0, : g.Ic]], axis=0)
    lbuf[d] = jnp.where(c == 0, both, turned) * dsg[...]
    for step in reversed(range(g.halvings - 1)):
        zsum.spread_wait(step + 1)
        zsum.spread_start(step)
    for k in range(1, g.T):
        columns(k).wait_send()
        column_in(k).wait_recv()

    def share(k):
        return [
            remote(cbuf.at[d], cbuf.at[d], send_s.at[0, k], recv_s.at[0, k], group(k)),
            remote(zbuf.at[d], zbuf.at[d], send_s.at[1, k], recv_s.at[1, k], group(k)),
            remote(lbuf.at[d], lbuf.at[d], send_s.at[2, k], recv_s.at[2, k], group(k)),
        ]

    def shared(k):
        other = flip(d, k, g.dbits)
        return [
            remote(cbuf.at[other], cbuf.at[other], send_s.at[0, k], recv_s.at[0, k], group(k)),
            remote(zbuf.at[other], zbuf.at[other], send_s.at[1, k], recv_s.at[1, k], group(k)),
            remote(lbuf.at[other], lbuf.at[other], send_s.at[2, k], recv_s.at[2, k], group(k)),
        ]

    for k in range(1, g.D):
        for item in share(k):
            item.start()
    for which, dst in ((0, ball), (1, tall)):
        local[which].wait()
        forward(which, dst, 0).start()
    for k in range(1, g.G):
        arrive(0, ball, k).wait_recv()
        forward(0, ball, k).start()
    for k in range(1, g.D):
        for item in share(k):
            item.wait_send()
        for item in shared(k):
            item.wait_recv()
    colall[...] = cbuf[...]
    zall[...] = zbuf[...]
    logall[...] = lbuf[...]
    for k in range(1, g.G):
        arrive(1, tall, k).wait_recv()
        forward(1, tall, k).start()
    zsum.spread_wait(0)
    zsum.sent()
    for which, src, dst in ((0, bout, ball), (1, tsend, tall)):
        for k in range(1, g.G):
            spread(which, src, dst, k).wait_send()
        for k in range(g.G):
            forward(which, dst, k).wait_send()
            arrive_forward(which, dst, k).wait_recv()


def wrap_kernel(g, colall, zall, logall, conds, dwm, dmb, drw, drb, dib, vectors):
    rows = []
    for member in range(g.T):
        rows.append(((member % 2) * g.G + member // 2) * g.Ro // g.L)
    value = conds[...]
    silu = value / (1.0 + jnp.exp(-value))
    picked = jnp.concatenate([silu[z, i : i + 1] for z in range(g.D) for i in rows], axis=0).astype(BF)
    twice = jnp.concatenate([picked, picked], axis=0)
    w = g.mw
    for row in range(6):
        part = jnp.concatenate(
            [colall[z, member, row : row + 1, :] for z in range(g.D) for member in range(g.T)], axis=0
        )
        dmb[row : row + 1, :] = jnp.sum(part, axis=0, keepdims=True)[:, :w]
        high = part.astype(BF)
        low = (part - high.astype(F32)).astype(BF)
        dwm[row * w : (row + 1) * w, :] = tn(jnp.concatenate([high, low], axis=0), twice)[:w]
    logits = jnp.concatenate([logall[z] for z in range(g.D)], axis=0)
    high = logits.astype(BF)
    low = (logits - high.astype(F32)).astype(BF)
    flat = jnp.concatenate([value[z] for z in range(g.D)], axis=0).astype(BF)
    router = tn(jnp.concatenate([high, low], axis=0), jnp.concatenate([flat, flat], axis=0))
    sums = jnp.sum(logits, axis=0, keepdims=True)
    for h in range(g.lh):
        drw[h] = router[2 * h : 2 * h + 2, :]
        drb[h : h + 1, :] = sums[:, 2 * h : 2 * h + 2]
    total = zall[0]
    for z in range(1, g.D):
        total = total + zall[z]
    dib[0:1, :] = total[1:2, : g.hw]
    dib[1:2, :] = total[1:2, 2 * g.hw : 3 * g.hw]
    vectors[...] = total


def body(
    groups, members,
    tokens, condition, timesteps, route_masks, modulate_weight, modulate_bias, input_weight, input_bias,
    output_weight, output_bias, expand_weight, expand_bias, reduce_weight, reduce_bias, router_weight, router_bias,
    out_cotangent,
):
    g = Plan(
        groups, members, tokens.shape[0], condition.shape[0], tokens.shape[1], router_weight.shape[1],
        modulate_weight.shape[2], input_weight.shape[2], expand_weight.shape[1],
    )
    dma = pltpu.SemaphoreType.DMA
    V = pltpu.VMEM
    W, T, G, D, I = g.W, g.T, g.G, g.D, g.I
    wide = 2 * g.lh
    wm = jnp.transpose(modulate_weight, (1, 2, 0)).reshape(6 * g.mw, W)
    wi = jnp.transpose(input_weight, (1, 2, 0)).reshape(3 * g.hw, W)
    we = expand_weight.T
    wr = reduce_weight
    rw = jnp.transpose(router_weight, (1, 2, 0))
    masks = jnp.transpose(route_masks, (1, 2, 0))
    eb = expand_bias.astype(F32)[None]
    ob = output_bias.astype(F32)[None]
    rbias = reduce_bias.astype(F32)[None]
    ru = g.ch // g.units

    mod, gat, dsg, smc, conds, wix, wex, wrx = call(
        functools.partial(start_kernel, g), "start",
        (condition, wm, modulate_bias, timesteps, masks, rw, router_bias, eb, input_bias, wi, we, wr),
        "vvvsvvvvvhhh",
        [
            ((6, I, W), F32), ((2, I, 128), F32), ((I, 128), F32), ((2, 8, W), F32), ((D, I, W), F32),
            ((3 * g.hw, W), BF), ((g.ch, W), BF), ((g.ch, W), BF),
        ],
        "vvvvvhhh",
        [
            V((T, I, 6 * g.mw), F32), V((2, I, 128), F32), V((2, 8, W), F32), V((D, I, W), F32),
            dma((T,)), dma((T,)), dma((5,)), dma((5,)), dma((D,)), dma((D,)),
        ],
        1,
    )
    h1, qkv, lse, att, res, h2, gath, wof = call(
        functools.partial(attend_kernel, g), "attend",
        (tokens, mod, gat, smc, wi, wix, output_weight, ob), "hvvvvvvv",
        [
            ((g.Rc, W), BF), ((wide * 3, g.hd, g.Rc), BF), ((wide, g.Rc), F32),
            ((g.Ro, W), F32), ((g.Ro, W), F32), ((g.Ro, W), BF), ((T * g.hw, g.Ro), BF), ((T * g.hw, W), BF),
        ],
        "vvvvvvvv",
        [
            V((g.Rc, W), BF), V((g.Ic, 2, g.hw, g.L), BF), V((T, g.hw, g.Ro), BF), V((T, g.hw, W), BF),
            dma, dma, dma((G,)), dma((G,)), dma((G,)), dma((G,)), dma((G,)), dma((G,)),
        ],
        2,
    )
    hgrad, mpart, dwf, small, gates, ebs = call(
        functools.partial(feed_kernel, g), "feed",
        (h2, out_cotangent, mod, gat, smc, we, wex, wr, wrx), "vhvvvhhhh",
        [
            ((g.Ro, W), F32), ((G, g.Ro, W), BF), ((2 * g.units, ru, W), BF),
            ((8, W), F32), ((2, 8, 128), F32), ((2, 8, W), F32),
        ],
        "vvvvvv",
        [
            V((g.Rc, W), BF), V((g.ch, W), BF), V((g.ch, W), BF), V((g.ch, W), BF), V((g.ch, W), BF),
            V((G, g.Ro, W), BF), V((g.Rc, W), BF), V((2, g.Rc, g.ch), BF), V((2, g.Rc, g.ch), BF),
            V((G - 1, g.Ro, W), BF), V((G - 1, g.Ro, W), BF), V((g.Ro, W), F32),
            V((2, g.ch, W), BF), V((2, g.ch, W), BF),
            dma((5,)), dma((G,)), dma((G,)), dma((G,)), dma((G,)), dma((2,)), dma((2,)),
        ],
        3,
    )
    grad, rgrad, bout, dwz, dwf, lines, sums, pay, gates = call(
        functools.partial(unattend_kernel, g), "unattend",
        (
            hgrad, h1, qkv, lse, gat, wi, wix, small, mpart, dwf, mod, att, res, wof, gath, out_cotangent, rbias, ebs,
            gates,
        ),
        "vvvvvvvvhhvvvvvhvvv",
        [
            ((g.Ro, W), F32), ((g.Ro, W), F32), ((g.Ro, W), BF), ((2 * g.units, g.zr, W), BF),
            ((2 * g.units, ru, W), BF), ((8, W), F32), ((8, W), F32), ((2, 8, W), F32), ((2, 8, 128), F32),
        ],
        "vvvvvvvvv",
        [
            V((T, g.hw, g.Ro), BF), V((G, 2, g.hw, g.Ro), BF), V((T, g.hw, W), BF), V((G, g.hw, W), BF),
            V((G, g.hw, W), BF), V((8, W), F32),
            V((2, 3 * g.hw, g.L), BF), V((2, 3 * g.hw, W), F32), V((g.Ro, W), F32), V((G - 1, g.Ro, W), BF),
            V((G - 1, g.Ro, W), BF), V((G, g.Ro, W), BF), V((3 * g.hw, W), BF), V((3 * g.hw, W), BF),
            V((G - 1, g.hw, W), BF), V((T, 8, W), F32), V((g.Ro, W), BF),
        ]
        + GroupSum.scratch(g, ru)
        + [
            dma((G,)), dma((G,)), dma((G,)), dma((G,)), dma((G,)), dma((G,)), dma((T,)), dma((T,)), dma, dma,
            dma((G,)), dma((G,)), dma((G,)), dma((G,)), dma((3,)),
        ],
        4,
    )
    tall, ball, colall, zall, logall, dwz = call(
        functools.partial(finish_kernel, g), "finish",
        (grad, rgrad, tokens, mod, lines, sums, bout, pay, gates, dsg, dwz), "vvhvvvvvvvv",
        [
            ((g.R, W), BF), ((g.R, W), BF), ((D, T, 8, g.cw), F32), ((D, 8, W), F32), ((D, I, 128), F32),
            ((2 * g.units, g.zr, W), BF),
        ],
        "hhvvvv",
        [
            V((g.Ro, W), BF), V((g.Ro, W), BF), V((T, 8, g.cw), F32), V((D, T, 8, g.cw), F32), V((D, 8, W), F32),
            V((D, I, 128), F32), V((8, W), F32), V((8, 128), F32),
        ]
        + GroupSum.scratch(g, g.zr)
        + [
            dma, dma((2, G)), dma((2, G)), dma((2, G)), dma((2, G)), dma((T,)), dma((T,)), dma((2,)), dma((2,)),
            dma((3, D)), dma((3, D)), dma((2,)),
        ],
        5,
    )
    dwm, dmb, drw, drb, dib, vectors = call(
        functools.partial(wrap_kernel, g), "wrap", (colall, zall, logall, conds), "vvvv",
        [
            ((6 * g.mw, W), F32), ((6, g.mw), F32), ((g.lh, 2, W), F32), ((g.lh, 2), F32), ((2, g.hw), F32),
            ((8, W), F32),
        ],
        "vvvvvv", [], None,
    )
    dwf = dwf.astype(F32).reshape(2, g.ch, W)
    dwz = dwz.astype(F32).reshape(4 * g.hw, W)
    return (
        ball.astype(F32),
        tall.astype(F32),
        jnp.transpose(dwm.reshape(6, g.mw, W), (2, 0, 1)),
        dmb,
        jnp.transpose(dwz[: 3 * g.hw].reshape(3, g.hw, W), (2, 0, 1)),
        dib,
        dwz[3 * g.hw :],
        vectors[2],
        dwf[1].T,
        vectors[0, : g.ch],
        dwf[0],
        vectors[3],
        jnp.transpose(drw, (2, 0, 1)),
        drb,
    )


def solution(mesh):
    return jax.shard_map(
        functools.partial(body, mesh.shape["dp"], mesh.shape["tensor"]),
        mesh=mesh,
        in_specs=(
            P("dp", None), P("dp", None), P("dp"), P(None, "tensor", None), P(None, None, "tensor"),
            P(None, "tensor"), P(None, None, "tensor"), P(None, "tensor"), P("tensor", None), P(),
            P(None, "tensor"), P("tensor"), P("tensor", None), P(), P(None, "tensor", None), P("tensor", None),
            P("dp", None),
        ),
        out_specs=(
            P("dp", None), P("dp", None), P(None, None, "tensor"), P(None, "tensor"), P(None, None, "tensor"),
            P(None, "tensor"), P("tensor", None), P(), P(None, "tensor"), P("tensor"), P("tensor", None), P(),
            P(None, "tensor", None), P("tensor", None),
        ),
        check_vma=False,
    )
```

time: 1140 us -> 304 us (0.27)
  waiting for transfers between devices: 788 us -> 0 us
  Pallas kernels: 0 us -> 281 us
  other arithmetic: 112 us -> 11.2 us
  matrix products: 84.4 us -> 0 us
  local copies, waits for them, and re-layouts: 78.2 us -> 10.6 us
  blocking collectives: 55.6 us -> 0 us
  between operations: 14.9 us -> 0.73 us
    psum x4 -> x0, waiting for transfers between devices: 788 us -> none  [the longest x1 341 us: body(): lax.psum((modulate_weight_grad, modulate_bias_grad, input_weight_grad, in...]
    pallas_call x0 -> x6, Pallas kernels: none -> 281 us  [call(): pl.pallas_call(kernel, name=name, out_shape=[jax.ShapeDtypeStruct(s, t) f...]
    dot_general x23 -> x0, matrix products: 84.4 us -> none  [the longest x3 16.9 us: contract_rows(): lax.dot_general(left, right, (((0,), (0,)), ((), ())), preferred_element_...]
    reduce_sum x14 -> x0, other arithmetic: 83.3 us -> none  [the longest x1 22.3 us: body(): scale_two_grad = jnp.sum(hidden_two_grad * normed_two, axis=1)]
    unnamed x144 -> x12, local copies, waits for them, and re-layouts: 51.5 us -> 0.32 us
    all_gather x1 -> x0, blocking collectives: 28.7 us -> none  [body(): modulation = lax.all_gather(modulate_part, 'tensor', axis=2, tiled=True)]
    psum x1 -> x0, blocking collectives: 26.9 us -> none  [body(): lax.psum((modulate_weight_grad, modulate_bias_grad, input_weight_grad, in...]
    add x3 -> x0, other arithmetic: 23 us -> none  [the longest x1 11.9 us: body(): residual_grad + norm_back(hidden_one_grad * (1.0 + scale_one), normed_one...]
  transfers between devices with their start and end apart: 4 -> 0, of which waited for: 4 -> 0; matrix products, arithmetic and copies ran while one was open for 10% -> 0% of each run, Pallas kernels for 0% -> 0%
where the time goes in v1:
time: 304 us
  Pallas kernels  281 us (92%)
  other arithmetic  11.2 us (4%)
  local copies, waits for them, and re-layouts  10.6 us (3%)
    pallas_call x6, Pallas kernels, call(): pl.pallas_call(kernel, name=name, out_shape=[jax.ShapeDtypeStruct(s, t) f...  281 us
    convert_element_type x1, other arithmetic, body(): ball.astype(F32)  6.84 us

profile of v1, /device:TPU:0, one launch (start us, length us, event | category | flops | bytes accessed | tf_op | source)
XLA Modules:
  0.0 303.9 jit_solution(8592910033802875706)
XLA Ops:
  0.6 1.3 reshape.53.eb
  1.9 0.0 copy-start.2
  1.9 14.6 %start.1 = (f32[6,8,1152]{2,1,0:T(8,128)}, f32[2,8,128]{2,1,0:T(8,128)}, f32[8,128]{1,0:T(8,128)}, f32[2,8,1152]{2,1,0:T(8,128)}, f32[4,8,1152]{2,1,0:T(8,128)},...) custom-call(f32[8,1152]{1,0:T(8,128)} %cond.1, bf16[864,1152]{1,0:T(8,128)(2,1)} %bitcast.30, ...), custom_call_target="tpu_custom_call" | custom-call | flops 100000000 | bytes 10000000 | tf_op jit(solution)/shard_map/start/pallas_call | solution.py:201
  16.5 0.0 copy-done.2
  16.5 0.6 reshape.54.ob
  17.1 33.6 %attend.1 = (bf16[1024,1152]{1,0:T(8,128)(2,1)}, bf16[12,72,1024]{2,1,0:T(8,128)(2,1)}, f32[4,1024]{1,0:T(4,128)}, f32[256,1152]{1,0:T(8,128)}, f32[256,1152]{1,...) custom-call(bf16[2048,1152]{1,0:T(8,128)(2,1)} %tokens.3, ...), custom_call_target="tpu_custom_call" | custom-call | flops 100000000 | bytes 10000000 | tf_op jit(solution)/shard_map/attend/pallas_call | solution.py:201
  50.7 0.0 copy-start.3
  50.7 58.8 %feed.1 = (f32[256,1152]{1,0:T(8,128)}, bf16[4,256,1152]{2,1,0:T(8,128)(2,1)}, bf16[8,144,1152]{2,1,0:T(8,128)(2,1)}, f32[8,1152]{1,0:T(8,128)}, f32[2,8,128]{2,1,0:T(8,128)}, /*index=5*/f32[2,8,1152]{2,1,0:T(8,128)}) custom-call(bf16[256,1152]{1,0:T(8,128)(2,1)} %get-tuple-element.61.h2, bf16[2048,1152]{1,0:T(8,128)(2,1)} %cotangent.3, ...), custom_call_target="tpu_custom_call" | custom-call | flops 100000000 | bytes 10000000 | tf_op jit(solution)/shard_map/feed/pallas_call | solution.py:201
  109.5 0.0 copy-done.3
  109.5 0.6 reshape.55.rbias
  110.1 104.1 %unattend.1 = (f32[256,1152]{1,0:T(8,128)}, f32[256,1152]{1,0:T(8,128)}, bf16[256,1152]{1,0:T(8,128)(2,1)}, bf16[8,72,1152]{2,1,0:T(8,128)(2,1)}, bf16[8,144,115...) custom-call(f32[256,1152]{1,0:T(8,128)} %get-tuple-element.64.hgrad,, ...), custom_call_target="tpu_custom_call" | custom-call | flops 100000000 | bytes 10000000 | tf_op jit(solution)/shard_map/unattend/pallas_call | solution.py:201
  214.2 66.1 %finish.1 = (bf16[2048,1152]{1,0:T(8,128)(2,1)}, bf16[2048,1152]{1,0:T(8,128)(2,1)}, f32[4,8,8,256]{3,2,1,0:T(8,128)}, f32[4,8,1152]{2,1,0:T(8,128)}, f32[4,8,12...) custom-call(f32[256,1152]{1,0:T(8,128)} %get-tuple-element.77.grad, f32[256,1152]{1,0:T(8,128)} %get-tuple-element.78.rgrad, ...), custom_call_target="tpu_custom_call" | custom-call | flops 100000000 | bytes 10000000 | tf_op jit(solution)/shard_map/finish/pallas_call | solution.py:201
  280.3 0.0 slice-start
  280.4 4.2 %wrap.1 = (f32[864,1152]{1,0:T(8,128)}, f32[6,144]{1,0:T(8,128)}, f32[2,2,1152]{2,1,0:T(2,128)}, f32[2,2]{1,0:T(2,128)}, f32[2,144]{1,0:T(2,128)}, /*index=5*/f32[8,1152]{1,0:T(8,128)}) custom-call(f32[4,8,8,256]{3,2,1,0:T(8,128)} %get-tuple-element.88.colall, f32[4,8,1152]{2,1,0:T(8,128)} %get-tuple-element.89.zall, f32[4,8,128]{2,1,0:T(8,128)} %get-tuple-element.90.logall, ...), custom_call_target="tpu_custom_call" | custom-call | flops 100000000 | bytes 10000000 | tf_op jit(solution)/shard_map/wrap/pallas_call | solution.py:201
  284.6 1.5 slice_reduce_fusion
  286.0 1.3 slice_reduce_fusion.2
  287.4 0.0 slice-start.1
  287.4 6.8 %convert_element_type.15 = f32[2048,1152]{1,0:T(8,128)} convert(bf16[2048,1152]{1,0:T(8,128)(2,1)} %get-tuple-element.86) | non-fusion elementwise | flops 2359296 | bytes 14155776 | tf_op jit(solution)/shard_map/convert_element_type | solution.py:1067
  294.2 0.0 slice-done
  294.2 0.0 slice-done.1
  294.2 0.0 copy-start.1
  294.2 4.4 %convert_element_type.16 = f32[2048,1152]{1,0:T(8,128)} convert(bf16[2048,1152]{1,0:T(8,128)(2,1)S(1)} %bitcast.27) | non-fusion elementwise | flops 2359296 | bytes 14155776 | tf_op jit(solution)/shard_map/convert_element_type | solution.py:1068
  298.6 0.0 copy-done.1
  298.6 0.0 copy-start
  298.6 1.4 slice.35
  300.0 0.9 slice.36
  300.9 0.3 copy-done
  301.2 2.7 fusion
  (1 shorter events, 0.0 us)
Async XLA Ops:
  1.9 14.6 %copy-start.2 = (bf16[1152]{0:T(1024)(128)(2,1)S(1)}, bf16[1152]{0:T(1024)(128)(2,1)}, u32[]{:S(2)}) copy-start(bf16[1152]{0:T(1024)(128)(2,1)} %param.26) | copy-start | bytes 6916
  50.7 58.8 %copy-start.3 = (bf16[1152]{0:T(1024)(128)(2,1)S(1)}, bf16[1152]{0:T(1024)(128)(2,1)}, u32[]{:S(2)}) copy-start(bf16[1152]{0:T(1024)(128)(2,1)} %param.30) | copy-start | bytes 6916
  280.3 13.9 %slice-start = ((s8[4718592]{0:T(1024)(128)(4,1)}), s8[524288]{0:T(1024)(128)(4,1)S(1)}, s32[]{:S(2)}) async-start(s8[4718592]{0:T(1024)(128)(4,1)} %bitcast.26), calls=%async_computation | async-start | bytes 1048576
  287.4 6.8 %slice-start.1 = ((s8[4718592]{0:T(1024)(128)(4,1)}), s8[4194304]{0:T(1024)(128)(4,1)S(1)}, s32[]{:S(2)}) async-start(s8[4718592]{0:T(1024)(128)(4,1)} %bitcast.26), calls=%async_computation.1 | async-start | bytes 8388608
  294.2 4.4 %copy-start.1 = (bf16[8,72,1152]{2,1,0:T(8,128)(2,1)S(1)}, bf16[8,72,1152]{2,1,0:T(8,128)(2,1)}, u32[]{:S(2)}) copy-start(bf16[8,72,1152]{2,1,0:T(8,128)(2,1)} %get-tuple-element.94) | copy-start | bytes 3981316
  298.6 2.6 copy-start

commit v2 on v1

--- a/solution.py
+++ b/solution.py
@@ -73,10 +73,11 @@
         self.ch = channels
         self.gc = channels // heads
         self.hr = 2 * headwidth
-        self.halvings = min(self.dbits, 2)
-        self.flips = [1, 3][: self.dbits] + [1 << b for b in range(2, self.dbits)]
-        self.units = 1 << self.halvings
-        self.zr = 4 * self.hw // (2 * self.units)
+        self.units = 8
+        self.fr = 2 * channels // self.units
+        self.zr = 4 * headwidth // self.units
+        self.fe = 2
+        self.ze = 4
 
     def place(self):
         d = lax.axis_index("dp")
@@ -91,6 +92,23 @@
     pl.semaphore_wait(barrier, len(devices))
 
 
+def meet_line(g, devices, group, middle):
+    barrier = pltpu.get_barrier_semaphore()
+    for device in devices + [group(1)]:
+        pl.semaphore_signal(barrier, inc=1, device_id=device, device_id_type=MESH)
+    others = [group(3)] + [group(4 << level) for level in range(g.dbits - 2)]
+
+    @pl.when(middle == 1)
+    def _():
+        for device in others:
+            pl.semaphore_signal(barrier, inc=1, device_id=device, device_id_type=MESH)
+        pl.semaphore_wait(barrier, len(devices) + 1 + len(others))
+
+    @pl.when(middle == 0)
+    def _():
+        pl.semaphore_wait(barrier, len(devices) + 1)
+
+
 def remote(src, dst, send, recv, device):
     return pltpu.make_async_remote_copy(
         src_ref=src, dst_ref=dst, send_sem=send, recv_sem=recv, device_id=device, device_id_type=MESH
@@ -98,96 +116,249 @@
 
 
 class GroupSum:
-    def __init__(self, g, work, inbox, full, send, recv, device):
-        self.g, self.work, self.inbox, self.full = g, work, inbox, full
-        self.send, self.recv, self.device = send, recv, device
+    def __init__(self, g, count, work, first, second, more, full, sems):
+        self.g, self.count, self.work, self.first, self.second = g, count, work, first, second
+        self.more, self.full, self.sems = more, full, sems
+        self.d, self.t = lax.axis_index("dp"), lax.axis_index("tensor")
+        self.middle = lax.rem(lax.rem(self.d, 4) + 1, 4) // 2
+
+    def device(self, mask):
+        return (flip(self.d, mask, self.g.dbits), self.t)
+
+    def copy(self, kind, src, dst, unit, mask):
+        return remote(src.at[unit], dst.at[unit], self.sems.at[kind, unit], self.sems.at[kind + 1, unit], self.device(mask))
+
+    def up(self, unit):
+        return self.copy(0, self.work, self.first, unit, 1)
+
+    def over(self, unit):
+        return self.copy(2, self.work, self.second, unit, 3)
+
+    def down(self, unit):
+        return self.copy(4, self.full, self.full, unit, 1)
+
+    def across(self, unit, level):
+        src = self.more.at[2 * level, unit]
+        dst = self.more.at[2 * level + 1, unit]
+        kind = 6 + 2 * level
+        return remote(src, dst, self.sems.at[kind, unit], self.sems.at[kind + 1, unit], self.device(4 << level))
+
+    def start(self, units):
+        @pl.when(self.middle == 0)
+        def _():
+            for unit in units:
+                self.up(unit).start()
+
+    def resume(self, units):
+        @pl.when(self.middle == 1)
+        def _():
+            for unit in units:
+                self.over(unit).start()
+
+    def join(self, units):
+        @pl.when(self.middle == 1)
+        def _():
+            for unit in units:
+                self.up(unit).wait_recv()
+                self.work[unit] = (self.work[unit].astype(F32) + self.first[unit].astype(F32)).astype(BF)
+                self.over(unit).start()
+
+    def settle(self, units):
+        @pl.when(self.middle == 1)
+        def _():
+            for unit in units:
+                self.over(unit).wait_recv()
+                value = (self.work[unit].astype(F32) + self.second[unit].astype(F32)).astype(BF)
+                for level in range(self.g.dbits - 2):
+                    self.more[2 * level, unit] = value
+                    copy = self.across(unit, level)
+                    copy.start()
+                    copy.wait()
+                    value = (value.astype(F32) + self.more[2 * level + 1, unit].astype(F32)).astype(BF)
+                self.full[unit] = value
+                self.down(unit).start()
+
+    def end(self, units, started):
+        @pl.when(self.middle == 0)
+        def _():
+            for unit in started:
+                self.up(unit).wait_send()
+            for unit in units:
+                self.down(unit).wait_recv()
+
+        @pl.when(self.middle == 1)
+        def _():
+            for unit in units:
+                self.over(unit).wait_send()
+                self.down(unit).wait_send()
+
+    @staticmethod
+    def scratch(g, count, rows):
+        levels = max(g.dbits - 2, 0)
+        return [
+            pltpu.VMEM((count, rows, g.W), BF), pltpu.VMEM((count, rows, g.W), BF), pltpu.VMEM((count, rows, g.W), BF),
+            pltpu.VMEM((max(2 * levels, 1), count if levels else 1, rows if levels else 16, g.W), BF),
+            pltpu.SemaphoreType.DMA((6 + 2 * levels, count)),
+        ]
+
+
+class FirstLeg:
+    def __init__(self, g, units, work, inbox, sems):
+        self.g, self.units, self.work, self.inbox, self.sems = g, units, work, inbox, sems
         d = lax.axis_index("dp")
-        low, high = lax.rem(d, 2), lax.rem(d // 2, 2)
-        both = low + high - 2 * low * high
-        self.steps = g.dbits
-        self.flips = [g.flips, g.flips[1::-1] + g.flips[2:]]
-        keeps = [[low], [low]] if g.dbits == 1 else [[both, high], [high, low]]
-        self.places = []
-        for which in range(2):
-            start, size, rows = which * g.units, g.units, []
-            for step in range(self.steps):
-                if step < g.halvings:
-                    half = size // 2
-                    keep = start + keeps[which][step] * half
-                    away = start + (1 - keeps[which][step]) * half
-                    rows.append((keep, away, half))
-                    start, size = keep, half
-                else:
-                    rows.append((start, start, size))
-            self.places.append(rows)
-
-    def peer(self, which, step):
-        return self.device(self.flips[which][step])
-
-    def box(self, which, step):
+        self.middle = lax.rem(lax.rem(d, 4) + 1, 4) // 2
+        self.other = (flip(d, 1, g.dbits), lax.axis_index("tensor"))
+
+    def copy(self, unit):
+        return remote(self.work.at[unit], self.inbox.at[unit], self.sems.at[0, unit], self.sems.at[1, unit], self.other)
+
+    def start(self):
+        @pl.when(self.middle == 0)
+        def _():
+            for unit in range(self.units):
+                self.copy(unit).start()
+
+    def add(self):
+        @pl.when(self.middle == 1)
+        def _():
+            for unit in range(self.units):
+                self.copy(unit).wait_recv()
+                self.work[unit] = (self.work[unit].astype(F32) + self.inbox[unit].astype(F32)).astype(BF)
+
+    def sent(self):
+        @pl.when(self.middle == 0)
+        def _():
+            for unit in range(self.units):
+                self.copy(unit).wait_send()
+
+    @staticmethod
+    def scratch(g, units, rows):
+        return [pltpu.VMEM((units, rows, g.W), BF), pltpu.SemaphoreType.DMA((2, units))]
+
+
+def half(g, ref, which):
+    return ref.at[pl.ds(which * (g.Ro // 2), g.Ro // 2)]
+
+
+class PlaneGather:
+    def __init__(self, g, src, place, send, recv, chip, p):
+        self.g, self.src, self.place, self.send, self.recv, self.chip, self.p = g, src, place, send, recv, chip, p
+        self.relayed = g.G == 4
+
+    def source(self, k):
+        return flip(self.p, k, self.g.bits)
+
+    def own(self, k, h):
         g = self.g
-        base = sum(g.units >> (s + 1) if s < g.halvings else 1 for s in range(step))
-        size = self.places[which][step][2]
-        return self.inbox.at[which, pl.ds(base, size)]
-
-    def copy(self, which, step):
-        _, away, size = self.places[which][step]
         return remote(
-            self.work.at[pl.ds(away, size)], self.box(which, step), self.send.at[which, step],
-            self.recv.at[which, step], self.peer(which, step),
+            half(g, self.src, h), half(g, self.place(k, self.p), h), self.send.at[k, h], self.recv.at[k, h], self.chip(k)
         )
 
-    def start(self, step):
-        for which in range(2):
-            self.copy(which, step).start()
-
-    def add(self, step):
-        for which in range(2):
-            keep, _, size = self.places[which][step]
-            copy = self.copy(which, step)
-            if step < self.g.halvings:
-                copy.wait_recv()
+    def arrival(self, k, h):
+        g = self.g
+        place = half(g, self.place(k, self.source(k)), h)
+        return remote(place, place, self.send.at[k, h], self.recv.at[k, h], self.chip(k))
+
+    def onward(self, h):
+        g = self.g
+        k = 1 + h
+        src = half(g, self.place(k, self.source(k)), h)
+        dst = half(g, self.place(3, self.source(k)), h)
+        return remote(src, dst, self.send.at[3, h], self.recv.at[3, h], self.chip(2 - h))
+
+    def start(self):
+        if self.relayed:
+            for k, h in ((1, 0), (2, 1), (1, 1), (2, 0)):
+                self.own(k, h).start()
+        else:
+            for k in range(1, self.g.G):
+                for h in range(2):
+                    self.own(k, h).start()
+
+    def relay(self):
+        if self.relayed:
+            for h in range(2):
+                self.arrival(1 + h, h).wait_recv()
+                self.onward(h).start()
+
+    def wait(self, k):
+        for h in range(2):
+            if not (self.relayed and k < 3 and h == k - 1):
+                self.arrival(k, h).wait_recv()
+
+    def sent(self):
+        for h in range(2):
+            for k in range(1, 3 if self.relayed else self.g.G):
+                self.own(k, h).wait_send()
+            if self.relayed:
+                self.onward(h).wait_send()
+
+
+class PlaneScatter:
+    def __init__(self, g, part, joint, final, send, recv, chip):
+        self.g, self.part, self.joint, self.final = g, part, joint, final
+        self.send, self.recv, self.chip = send, recv, chip
+        self.relayed = g.G == 4
+
+    def far(self, h):
+        return remote(
+            half(self.g, self.part(3), h), self.joint.at[h], self.send.at[2, h], self.recv.at[2, h], self.chip(1 + h)
+        )
+
+    def near(self, k, h):
+        g = self.g
+        return remote(
+            half(g, self.part(k), h), half(g, self.final.at[k - 1], h), self.send.at[k - 1, h], self.recv.at[k - 1, h],
+            self.chip(k),
+        )
+
+    def put(self, k):
+        if not self.relayed:
+            for h in range(2):
+                self.near(k, h).start()
+        elif isinstance(k, int):
+            if k == 3:
+                self.far(0).start()
+                self.far(1).start()
             else:
-                copy.wait()
-            rows = pl.ds(keep, size)
-            self.work[rows] = (self.work[rows].astype(F32) + self.box(which, step)[...].astype(F32)).astype(BF)
+                self.near(k, k - 1).start()
+        else:
+            for kk in range(1, 4):
+
+                @pl.when(k == kk)
+                def _():
+                    self.put(kk)
+
+    def join(self):
+        if self.relayed:
+            for h in range(2):
+                k = 2 - h
+                self.far(h).wait_recv()
+                rows = pl.ds(h * (self.g.Ro // 2), self.g.Ro // 2)
+                ref = self.part(k)
+                ref[rows] = (ref[rows].astype(F32) + self.joint[h].astype(F32)).astype(BF)
+                self.near(k, h).start()
+
+    def total(self, value):
+        for k in range(1, 3 if self.relayed else self.g.G):
+            for h in range(2):
+                self.near(k, h).wait_recv()
+            value = value + self.final[k - 1].astype(F32)
+        return value
 
     def sent(self):
-        for step in range(self.g.halvings):
-            for which in range(2):
-                self.copy(which, step).wait_send()
-
-    def spread(self, which, step):
-        keep, _, size = self.places[which][step]
-        rows = self.full.at[pl.ds(keep, size)]
-        slot = self.steps + step
-        return remote(rows, rows, self.send.at[which, slot], self.recv.at[which, slot], self.peer(which, step))
-
-    def gathered(self, which, step):
-        _, away, size = self.places[which][step]
-        rows = self.full.at[pl.ds(away, size)]
-        slot = self.steps + step
-        return remote(rows, rows, self.send.at[which, slot], self.recv.at[which, slot], self.peer(which, step))
-
-    def spread_start(self, step):
-        for which in range(2):
-            if step == self.g.halvings - 1:
-                keep, _, size = self.places[which][step]
-                self.full[pl.ds(keep, size)] = self.work[pl.ds(keep, size)]
-            self.spread(which, step).start()
-
-    def spread_wait(self, step):
-        for which in range(2):
-            self.spread(which, step).wait_send()
-            self.gathered(which, step).wait_recv()
+        for h in range(2):
+            for k in range(1, 3 if self.relayed else self.g.G):
+                self.near(k, h).wait_send()
+            if self.relayed:
+                self.far(h).wait_send()
 
     @staticmethod
-    def scratch(g, rows):
-        boxes = sum(g.units >> (s + 1) if s < g.halvings else 1 for s in range(g.dbits))
+    def scratch(g):
         dma = pltpu.SemaphoreType.DMA
         return [
-            pltpu.VMEM((2 * g.units, rows, g.W), BF), pltpu.VMEM((2, boxes, rows, g.W), BF),
-            dma((2, 2 * g.dbits)), dma((2, 2 * g.dbits)),
+            pltpu.VMEM((2, g.Ro // 2, g.W), BF), pltpu.VMEM((2 if g.G == 4 else g.G - 1, g.Ro, g.W), BF),
+            dma((g.G, 2)), dma((g.G, 2)),
         ]
 
 
@@ -297,12 +468,14 @@
 
 def attend_kernel(
     g, tokens, mod, gat, smc, wi, wix, wo, ob,
-    h1, qkv, lse, att, res, h2, gath, wof,
-    tok, gsend, gbuf, wob, load, keep, send, recv, send_o, recv_o, send_f, recv_f,
+    h1_out, qkv_out, lse, att, res, h2, gath, wof,
+    tok, h1, qkv, gsend, gbuf, wob, load, keep, save, send, recv, send_o, recv_o, send_f, recv_f,
 ):
     d, t, p, c = g.place()
     partner = (d, p * 2 + 1 - c)
     weights = (wi, wix)
+    copy = pltpu.make_async_copy(tokens.at[pl.ds(pl.multiple_of(c * g.Rc, g.Rc), g.Rc)], tok, load)
+    copy.start()
     meet([(d, flip(p, k, g.bits) * 2 + c) for k in range(1, g.G)] + [partner])
 
     def share(k):
@@ -317,8 +490,6 @@
         share(k).start()
     forward(0).start()
     wob[t] = wo[...]
-    copy = pltpu.make_async_copy(tokens.at[pl.ds(pl.multiple_of(c * g.Rc, g.Rc), g.Rc)], tok, load)
-    copy.start()
     copy.wait()
     scale = 1.0 / math.sqrt(g.hd)
     ones = jnp.ones((8, g.L), BF)
@@ -345,6 +516,13 @@
         i = flip(p // g.sub, g.Ic - 1 - ii, g.bits)
         rows = pl.ds(pl.multiple_of(i * g.L, g.L), g.L)
         row = c * g.Ic + i
+
+        @pl.when(ii == g.Ic - 1)
+        def _():
+            for k in range(1, g.G):
+                share(k).wait_recv()
+                forward(k).start()
+
         normed, _ = norm(tok[rows].astype(F32))
         hidden = (
             normed * (1.0 + mod[1, pl.ds(row, 1), :]) + mod[0, pl.ds(row, 1), :]
@@ -391,18 +569,19 @@
         return carry
 
     lax.fori_loop(0, g.Ic, item, 0)
+    saves = [pltpu.make_async_copy(h1, h1_out, save.at[0]), pltpu.make_async_copy(qkv, qkv_out, save.at[1])]
+    for copy in saves:
+        copy.start()
     home().wait()
     for k in range(1, g.G):
         arrive(flip(p, k, g.bits)).wait_recv()
     heads = gbuf[...].reshape(g.T * g.hw, g.Ro)
     gath[...] = heads
-    for k in range(1, g.G):
-        share(k).wait_recv()
-        forward(k).start()
     for k in range(g.G):
         forward(k).wait_recv()
+    saves.append(pltpu.make_async_copy(wob, wof, save.at[2]))
+    saves[-1].start()
     full = wob[...].reshape(g.T * g.hw, g.W)
-    wof[...] = full
     attention = tn(heads, full) + ob[...]
     own = c * g.Ic + p // g.sub
     base = tok[pl.ds(pl.multiple_of(p * g.Ro, g.Ro), g.Ro)].astype(F32)
@@ -416,13 +595,15 @@
         share(k).wait_send()
     for k in range(g.G):
         forward(k).wait_send()
+    for copy in saves:
+        copy.wait()
 
 
 def feed_kernel(
     g, h2, cotangent, mod, gat, smc, we_in, wex_in, wr_in, wrx_in,
-    grad_out, mpart, dwf, small, gates, ebs,
-    cot, we, wex, wr, wrx, h2buf, bgbuf, gch, egb, sgb, rgb, own_g, xs, xr,
-    load, send_h, recv_h, send_g, recv_g, send_p, recv_p,
+    grad_out, mpart_out, dwf_out, small, gates, ebs,
+    cot, we, wex, wr, wrx, h2buf, bgbuf, gch, egb, sgb, own_g, xs, xr, mpart, dwf,
+    joint, final, send_g, recv_g, leg_box, leg_sems, done, load, save, send_h, recv_h, send_p, recv_p,
 ):
     d, t, p, c = g.place()
     partner = (d, p * 2 + 1 - c)
@@ -441,13 +622,12 @@
     ]
     for copy in loads:
         copy.start()
-    meet([chip(k) for k in range(1, g.G)] + [partner])
-
-    def spread(k):
-        return remote(h2, h2buf.at[k], send_h.at[k], recv_h.at[k], chip(k))
-
-    for k in range(1, g.G):
-        spread(k).start()
+    leg = FirstLeg(g, g.fe, dwf, leg_box, leg_sems)
+    meet([chip(k) for k in range(1, g.G)] + [partner, leg.other])
+
+    spread = PlaneGather(g, h2, lambda k, source: h2buf.at[k], send_h, recv_h, chip, p)
+    spread.start()
+    back = PlaneScatter(g, lambda k: sgb.at[k - 1], joint, final, send_g, recv_g, chip)
     h2buf[0] = h2[...]
     for copy in loads:
         copy.wait()
@@ -456,9 +636,6 @@
     tile_lane = lax.broadcasted_iota(jnp.int32, (8, 128), 1)
     ebs[...] = jnp.zeros_like(ebs)
     gates[...] = jnp.zeros_like(gates)
-
-    def back(k):
-        return remote(sgb.at[k - 1], rgb.at[k - 1], send_g.at[k], recv_g.at[k], chip(k))
 
     def block(k, carry):
         j = flip(p, k, g.bits)
@@ -470,9 +647,15 @@
         bgbuf[here] = branch
         grads = [nt(branch, wrc[s][...]) for s in range(2)]
 
-        @pl.when(k > 0)
-        def _():
-            spread(k).wait_recv()
+        @pl.when(k == 1)
+        def _():
+            spread.relay()
+
+        for kk in range(1, g.G):
+
+            @pl.when(k == kk)
+            def _():
+                spread.wait(kk)
 
         hidden = h2buf[k]
         total = None
@@ -504,7 +687,7 @@
         @pl.when(k > 0)
         def _():
             sgb[k - 1] = total.astype(BF)
-            back(k).start()
+            back.put(k)
 
         @pl.when(k == 0)
         def _():
@@ -513,47 +696,64 @@
         return carry
 
     lax.fori_loop(0, g.G, block, 0)
-    xs[0] = tn(gch[1], bgbuf[...]).astype(BF)
-
     def swap(index):
         return remote(xs.at[index], xr.at[index], send_p.at[index], recv_p.at[index], partner)
 
-    swap(0).start()
-    xs[1] = tn(egb[1], h2buf[...].reshape(g.Rc, g.W)).astype(BF)
-    swap(1).start()
-    unit = g.ch // g.units
-    for index, (left, right) in enumerate(
-        ((gch[0], bgbuf[...]), (egb[0], h2buf[...].reshape(g.Rc, g.W)))
-    ):
-        value = tn(left, right)
+    half_units = g.units // 2
+    saves = []
+    for index, left in enumerate((gch, egb)):
+        right = bgbuf[...] if index == 0 else h2buf[...].reshape(g.Rc, g.W)
+        xs[index] = tn(left[1], right).astype(BF)
+        swap(index).start()
+        value = tn(left[0], right)
         swap(index).wait_recv()
         value = (value + xr[index].astype(F32)).astype(BF)
-        for u in range(g.units):
-            dwf[index * g.units + u] = value[u * unit : (u + 1) * unit]
+        for u in range(half_units):
+            dwf[index * half_units + u] = value[u * g.fr : (u + 1) * g.fr]
+        if index == 0:
+            leg.start()
+            back.join()
+    copy = pltpu.make_async_copy(dwf.at[pl.ds(g.fe, g.units - g.fe)], dwf_out.at[pl.ds(g.fe, g.units - g.fe)], save.at[0])
+    copy.start()
+    saves.append(copy)
     for k in range(g.G):
         rows = pl.ds(k * g.Ro, g.Ro)
         mpart[k] = (nn(gch[0, rows], wr[...]) + nn(gch[1, rows], wrx[...])).astype(BF)
+    saves.append(pltpu.make_async_copy(mpart, mpart_out, save.at[2]))
+    saves[-1].start()
     small[...] = jnp.zeros_like(small)
     small[7:8, :] = jnp.sum(bgbuf[0 : g.Ro].astype(F32), axis=0, keepdims=True)
-    grad = own_g[...]
-    for k in range(1, g.G):
-        back(k).wait_recv()
-        grad = grad + rgb[k - 1].astype(F32)
-    grad_out[...] = grad
-    for k in range(1, g.G):
-        spread(k).wait_send()
-        back(k).wait_send()
+    grad_out[...] = back.total(own_g[...])
+    leg.add()
+    copy = pltpu.make_async_copy(dwf.at[pl.ds(0, g.fe)], dwf_out.at[pl.ds(0, g.fe)], save.at[1])
+    copy.start()
+    saves.append(copy)
+    leg.sent()
+
+    @pl.when(leg.middle == 1)
+    def _():
+        pl.semaphore_signal(done, inc=1, device_id=leg.other, device_id_type=MESH)
+
+    @pl.when(leg.middle == 0)
+    def _():
+        pl.semaphore_wait(done, 1)
+
+    spread.sent()
+    back.sent()
     swap(0).wait_send()
     swap(1).wait_send()
+    for copy in saves:
+        copy.wait()
 
 
 def unattend_kernel(
-    g, hgrad, h1, qkv, lse, gat, wi, wix, small_in, mpart, dwf, mod, att, res, wof, gath, cotangent, rbias, ebs,
-    gates_in,
+    g, hgrad, h1_in, qkv_in, lse, gat, wi_in, wix_in, small_in, mpart_in, dwf, mod, att, res, wof_in, gath_in,
+    cotangent, rbias, ebs, gates_in,
     grad, rgrad, bout, dwz, dwf_out, lines, sums, pay, gates,
-    hgs, hgbuf, wof_x, orr, osum, small, dqkv, acc, own_g, sgb, rgb, rmb, xs, xr, orv, sx, cot,
-    work, inbox, send_z, recv_z,
-    send_g, recv_g, send_m, recv_m, send_o, recv_o, send_s, recv_s, send_p, recv_p, send_a, recv_a, send_x, recv_x,
+    h1, qkv, wi, wix, mpart, wof, gath,
+    hgs, hgbuf, wof_x, orr, osum, small, dqkv, acc, own_g, sgb, xs, xr, orv, sx, cot,
+    work, first_z, second_z, more_z, sems_z, leg_box, leg_sems, joint_g, final_g, send_g, recv_g, joint_m, final_m, send_m, recv_m,
+    send_o, recv_o, send_s, recv_s, send_p, recv_p, send_a, recv_a, send_x, recv_x,
     load,
 ):
     d, t, p, c = g.place()
@@ -576,15 +776,25 @@
     fetch.start()
     half = pltpu.make_async_copy(dwf, work, load.at[1])
     half.start()
-    first = pltpu.make_async_copy(mpart.at[0], rmb.at[0], load.at[2])
-    first.start()
-    meet([peer(k) for k in range(1, g.T)] + [group(k) for k in g.flips])
+    loads = [
+        pltpu.make_async_copy(src, dst, load.at[2 + index])
+        for index, (src, dst) in enumerate(
+            (
+                (wof_in, wof), (mpart_in, mpart), (gath_in, gath), (h1_in, h1), (qkv_in, qkv), (wi_in, wi),
+                (wix_in, wix),
+            )
+        )
+    ]
+    for copy in loads:
+        copy.start()
+    zsum = GroupSum(g, g.units, work, first_z, second_z, more_z, dwf_out, sems_z)
+    meet_line(g, [peer(k) for k in range(1, g.T)], group, zsum.middle)
 
     def rest(k):
         return remote(osum.at[flip(p, k, g.bits)], orv.at[k - 1], send_o.at[k], recv_o.at[k], chip(k))
 
-    def on(k):
-        return remote(mpart.at[k], rmb.at[k], send_m.at[k], recv_m.at[k], chip(k))
+    on = PlaneScatter(g, lambda k: mpart.at[k], joint_m, final_m, send_m, recv_m, chip)
+    back = PlaneScatter(g, lambda k: sgb.at[k - 1], joint_g, final_g, send_g, recv_g, chip)
 
     def sumup(k):
         return remote(small, sx.at[k], send_s.at[k], recv_s.at[k], peer(k))
@@ -596,8 +806,10 @@
         return remote(wof_x.at[2 * q + 1 - c], orr.at[q], send_x.at[q], recv_x.at[q], partner)
 
     half.wait()
-    zsum = GroupSum(g, work, inbox, dwf_out, send_z, recv_z, group)
-    zsum.start(0)
+    everything = list(range(g.units))
+    zsum.resume(everything[: g.fe])
+    zsum.start(everything[g.fe :])
+    leg = FirstLeg(g, g.ze, dwz, leg_box, leg_sems)
     fetch.wait()
     value = hgrad[...]
     own = c * g.Ic + p // g.sub
@@ -605,12 +817,14 @@
     cot_own = cot[...].astype(F32)
     residual = cot_own + norm_back(value * (1.0 + mod[4, pl.ds(own, 1), :]), normed, inverse)
     branch_one = (mod[2, pl.ds(own, 1), :] * residual).astype(BF)
+    loads[0].wait()
     hgs[...] = nt(wof[...], branch_one).astype(BF).reshape(g.T, g.hw, g.Ro)
-    for k in range(1, g.G):
+    for k in reversed(range(1, g.G)):
         heads_out(k).start()
     hgbuf[0] = hgs[pl.ds(p * 2, 2)]
-    for k in range(1, g.G):
-        on(k).start()
+    loads[1].wait()
+    for k in reversed(range(1, g.G)):
+        on.put(k)
     rgrad[...] = residual
     small[...] = small_in[...]
     small[2:3, :] = jnp.sum(residual * att[...], axis=0, keepdims=True)
@@ -619,6 +833,8 @@
     small[6:7, :] = jnp.sum(branch_one.astype(F32), axis=0, keepdims=True)
     for k in range(1, g.T):
         sumup(k).start()
+    for copy in loads[2:]:
+        copy.wait()
     wof_x[...] = nn(gath[...], branch_one).astype(BF).reshape(g.T, g.hw, g.W)
     for q in range(g.G):
         cross(q).start()
@@ -630,14 +846,12 @@
     gates[...] = gates_in[...]
     pay[...] = ebs[...]
 
-    def back(k):
-        return remote(sgb.at[k - 1], rgb.at[k - 1], send_g.at[k], recv_g.at[k], chip(k))
-
     def item(ii, carry):
-        i = flip(p // g.sub, ii, g.bits)
+        kk = lax.rem(g.Ic - ii, g.Ic)
+        i = flip(p // g.sub, kk, g.bits)
         row = c * g.Ic + i
         rows = pl.ds(pl.multiple_of(i * g.L, g.L), g.L)
-        slots = [ii * g.sub + (flip(lax.rem(p, g.sub), u, 4) if g.sub > 1 else 0) for u in range(g.sub)]
+        slots = [kk * g.sub + (flip(lax.rem(p, g.sub), u, 4) if g.sub > 1 else 0) for u in range(g.sub)]
         hidden = h1[rows]
         total = None
         for u, slot in enumerate(slots):
@@ -646,8 +860,15 @@
             def _():
                 heads_out(slot).wait_recv()
 
+        @pl.when(ii == min(2, g.Ic - 1))
+        def _():
+            zsum.settle([1])
+            zsum.join([3])
+
         @pl.when(ii == 1)
         def _():
+            zsum.settle([0])
+            zsum.join([2])
             for q in range(g.G):
                 cross(q).wait()
                 osum[q] = (wof_x[2 * q + c].astype(F32) + orr[q].astype(F32)).astype(BF)
@@ -656,9 +877,7 @@
 
         @pl.when(ii == g.Ic - 1)
         def _():
-            zsum.add(0)
-            if g.dbits > 1:
-                zsum.start(1)
+            on.join()
 
         for s in range(2):
             core = c + s - 2 * c * s
@@ -701,7 +920,7 @@
             @pl.when(slot != 0)
             def _():
                 sgb[slot - 1] = piece.astype(BF)
-                back(slot).start()
+                back.put(slot)
 
         return carry
 
@@ -709,11 +928,22 @@
     xs[...] = acc[1].astype(BF)
     swap = remote(xs, xr, send_p, recv_p, partner)
     swap.start()
-    for step in range(1, g.dbits):
-        zsum.add(step)
-        if step + 1 < g.dbits:
-            zsum.start(step + 1)
-    zsum.spread_start(g.halvings - 1)
+    zsum.settle([2])
+    zsum.join([4])
+    swap.wait()
+    for u in range(g.units):
+        low = u * g.zr
+        if low < 3 * g.hw:
+            span = slice(low, low + g.zr)
+            dwz[u] = (acc[0, span] + xr[span].astype(F32)).astype(BF)
+    leg.start()
+    zsum.settle([3])
+    zsum.join([5])
+    zsum.settle([4])
+    zsum.join([6])
+    back.join()
+    zsum.settle([5])
+    zsum.join([7])
     value = small[...]
     for k in range(1, g.T):
         sumup(k).wait()
@@ -723,33 +953,22 @@
     for k in range(1, g.G):
         rest(k).wait()
         out = out + orv[k - 1].astype(F32)
-    swap.wait()
-    for u in range(2 * g.units):
+    for u in range(g.units):
         low = u * g.zr
-        if low < 3 * g.hw:
-            span = slice(low, low + g.zr)
-            dwz[u] = (acc[0, span] + xr[span].astype(F32)).astype(BF)
-        else:
+        if low >= 3 * g.hw:
             dwz[u] = out[low - 3 * g.hw : low - 3 * g.hw + g.zr].astype(BF)
-    for step in reversed(range(g.halvings - 1)):
-        zsum.spread_wait(step + 1)
-        zsum.spread_start(step)
-    first.wait()
-    branch = rmb[0].astype(F32)
-    for k in range(1, g.G):
-        on(k).wait()
-        branch = branch + rmb[k].astype(F32)
-    branch = branch + rbias[...]
+    zsum.settle([6])
+    branch = on.total(mpart[0].astype(F32)) + rbias[...]
     bout[...] = (res[...] + mod[5, pl.ds(own, 1), :] * branch).astype(BF)
     lines[...] = small[...]
     lines[5:6, :] = jnp.sum(cot[...].astype(F32) * branch, axis=0, keepdims=True)
-    value = own_g[...]
-    for k in range(1, g.G):
-        back(k).wait()
-        value = value + rgb[k - 1].astype(F32)
-    grad[...] = value
-    zsum.spread_wait(0)
-    zsum.sent()
+    grad[...] = back.total(own_g[...])
+    on.sent()
+    back.sent()
+    zsum.settle([7])
+    leg.add()
+    zsum.end(everything, everything[g.fe :])
+    leg.sent()
     for k in range(1, g.G):
         heads_out(k).wait_send()
 
@@ -757,7 +976,7 @@
 def finish_kernel(
     g, grad, rgrad, tokens, mod, lines_in, sums, bout, pay, gates, dsg, dwz,
     tall, ball, colall, zall, logall, dwz_out,
-    tok, tsend, stage, cbuf, zbuf, lbuf, pbuf, gbuf, work, inbox, send_z, recv_z,
+    tok, tsend, stage, cbuf, zbuf, lbuf, pbuf, gbuf, work, first_z, second_z, more_z, sems_z,
     load, send_t, recv_t, send_f, recv_f, send_c, recv_c, send_p, recv_p, send_s, recv_s, keep,
 ):
     d, t, p, c = g.place()
@@ -783,15 +1002,18 @@
     ]
     for swap in swaps:
         swap.start()
-    zsum = GroupSum(g, work, inbox, dwz_out, send_z, recv_z, group)
+    zsum = GroupSum(g, g.units, work, first_z, second_z, more_z, dwz_out, sems_z)
+    everything = list(range(g.units))
     work[...] = dwz[...]
-    zsum.start(0)
-
-    def spread(which, src, dst, k):
-        return remote(src, dst.at[mine], send_t.at[which, k], recv_t.at[which, k], chip(k))
-
-    for k in range(1, g.G):
-        spread(0, bout, ball, k).start()
+    zsum.resume(everything[: g.ze])
+    zsum.start(everything[g.ze :])
+
+    def rows_of(dst):
+        return lambda k, source: dst.at[pl.ds(pl.multiple_of((c * g.G + source) * g.Ro, g.Ro), g.Ro)]
+
+    outs = PlaneGather(g, bout, rows_of(ball), send_t.at[0], recv_t.at[0], chip, p)
+    grads = PlaneGather(g, tsend, rows_of(tall), send_t.at[1], recv_t.at[1], chip, p)
+    outs.start()
     copy.wait()
     own = c * g.Ic + p // g.sub
     normed, inverse = norm(tok[...].astype(F32))
@@ -817,8 +1039,7 @@
     for k in range(1, g.T):
         columns(k).start()
     cbuf[d, t] = stage[t]
-    for k in range(1, g.G):
-        spread(1, tsend, tall, k).start()
+    grads.start()
     local = [
         pltpu.make_async_copy(bout, ball.at[mine], keep.at[0]),
         pltpu.make_async_copy(tsend, tall.at[mine], keep.at[1]),
@@ -830,19 +1051,13 @@
         rows = pl.ds(pl.multiple_of((c * g.G + flip(p, k, g.bits)) * g.Ro, g.Ro), g.Ro)
         return remote(dst.at[rows], dst.at[rows], send_f.at[which, k], recv_f.at[which, k], partner)
 
-    def arrive(which, dst, k):
-        rows = pl.ds(pl.multiple_of((c * g.G + flip(p, k, g.bits)) * g.Ro, g.Ro), g.Ro)
-        return remote(bout, dst.at[rows], send_t.at[which, k], recv_t.at[which, k], chip(k))
-
     def arrive_forward(which, dst, k):
         rows = pl.ds(pl.multiple_of(((1 - c) * g.G + flip(p, k, g.bits)) * g.Ro, g.Ro), g.Ro)
         return remote(dst.at[rows], dst.at[rows], send_f.at[which, k], recv_f.at[which, k], partner)
 
-    for step in range(g.dbits):
-        zsum.add(step)
-        if step + 1 < g.dbits:
-            zsum.start(step + 1)
-    zsum.spread_start(g.halvings - 1)
+    outs.relay()
+    zsum.join([4])
+    zsum.settle([0, 1])
     for swap in swaps:
         swap.wait()
     zbuf[d] = jnp.zeros((8, g.W), F32)
@@ -851,9 +1066,8 @@
     both = jnp.concatenate([gates[0, : g.Ic], gbuf[: g.Ic]], axis=0)
     turned = jnp.concatenate([gbuf[: g.Ic], gates[0, : g.Ic]], axis=0)
     lbuf[d] = jnp.where(c == 0, both, turned) * dsg[...]
-    for step in reversed(range(g.halvings - 1)):
-        zsum.spread_wait(step + 1)
-        zsum.spread_start(step)
+    zsum.join([5, 6])
+    zsum.settle([2])
     for k in range(1, g.T):
         columns(k).wait_send()
         column_in(k).wait_recv()
@@ -879,8 +1093,12 @@
     for which, dst in ((0, ball), (1, tall)):
         local[which].wait()
         forward(which, dst, 0).start()
+    zsum.join([7])
+    zsum.settle([3, 4])
+    grads.relay()
+    zsum.settle([5, 6, 7])
     for k in range(1, g.G):
-        arrive(0, ball, k).wait_recv()
+        outs.wait(k)
         forward(0, ball, k).start()
     for k in range(1, g.D):
         for item in share(k):
@@ -891,13 +1109,12 @@
     zall[...] = zbuf[...]
     logall[...] = lbuf[...]
     for k in range(1, g.G):
-        arrive(1, tall, k).wait_recv()
+        grads.wait(k)
         forward(1, tall, k).start()
-    zsum.spread_wait(0)
-    zsum.sent()
-    for which, src, dst in ((0, bout, ball), (1, tsend, tall)):
-        for k in range(1, g.G):
-            spread(which, src, dst, k).wait_send()
+    zsum.end(everything, everything[g.ze :])
+    outs.sent()
+    grads.sent()
+    for which, dst in ((0, ball), (1, tall)):
         for k in range(g.G):
             forward(which, dst, k).wait_send()
             arrive_forward(which, dst, k).wait_recv()
@@ -960,7 +1177,6 @@
     eb = expand_bias.astype(F32)[None]
     ob = output_bias.astype(F32)[None]
     rbias = reduce_bias.astype(F32)[None]
-    ru = g.ch // g.units
 
     mod, gat, dsg, smc, conds, wix, wex, wrx = call(
         functools.partial(start_kernel, g), "start",
@@ -982,12 +1198,12 @@
         (tokens, mod, gat, smc, wi, wix, output_weight, ob), "hvvvvvvv",
         [
             ((g.Rc, W), BF), ((wide * 3, g.hd, g.Rc), BF), ((wide, g.Rc), F32),
-            ((g.Ro, W), F32), ((g.Ro, W), F32), ((g.Ro, W), BF), ((T * g.hw, g.Ro), BF), ((T * g.hw, W), BF),
+            ((g.Ro, W), F32), ((g.Ro, W), F32), ((g.Ro, W), BF), ((T * g.hw, g.Ro), BF), ((T, g.hw, W), BF),
         ],
-        "vvvvvvvv",
+        "hhvvvvvh",
         [
-            V((g.Rc, W), BF), V((g.Ic, 2, g.hw, g.L), BF), V((T, g.hw, g.Ro), BF), V((T, g.hw, W), BF),
-            dma, dma, dma((G,)), dma((G,)), dma((G,)), dma((G,)), dma((G,)), dma((G,)),
+            V((g.Rc, W), BF), V((g.Rc, W), BF), V((wide * 3, g.hd, g.Rc), BF), V((g.Ic, 2, g.hw, g.L), BF), V((T, g.hw, g.Ro), BF), V((T, g.hw, W), BF),
+            dma, dma, dma((3,)), dma((G,)), dma((G,)), dma((G,)), dma((G,)), dma((G,)), dma((G,)),
         ],
         2,
     )
@@ -995,42 +1211,49 @@
         functools.partial(feed_kernel, g), "feed",
         (h2, out_cotangent, mod, gat, smc, we, wex, wr, wrx), "vhvvvhhhh",
         [
-            ((g.Ro, W), F32), ((G, g.Ro, W), BF), ((2 * g.units, ru, W), BF),
+            ((g.Ro, W), F32), ((G, g.Ro, W), BF), ((g.units, g.fr, W), BF),
             ((8, W), F32), ((2, 8, 128), F32), ((2, 8, W), F32),
         ],
-        "vvvvvv",
+        "vhhvvv",
         [
             V((g.Rc, W), BF), V((g.ch, W), BF), V((g.ch, W), BF), V((g.ch, W), BF), V((g.ch, W), BF),
             V((G, g.Ro, W), BF), V((g.Rc, W), BF), V((2, g.Rc, g.ch), BF), V((2, g.Rc, g.ch), BF),
-            V((G - 1, g.Ro, W), BF), V((G - 1, g.Ro, W), BF), V((g.Ro, W), F32),
-            V((2, g.ch, W), BF), V((2, g.ch, W), BF),
-            dma((5,)), dma((G,)), dma((G,)), dma((G,)), dma((G,)), dma((2,)), dma((2,)),
-        ],
+            V((G - 1, g.Ro, W), BF), V((g.Ro, W), F32),
+            V((2, g.ch, W), BF), V((2, g.ch, W), BF), V((G, g.Ro, W), BF), V((g.units, g.fr, W), BF),
+        ]
+        + PlaneScatter.scratch(g)
+        + FirstLeg.scratch(g, g.fe, g.fr)
+        + [pltpu.SemaphoreType.REGULAR, dma((5,)), dma((3,)), dma((G, 2)), dma((G, 2)), dma((2,)), dma((2,))],
         3,
     )
     grad, rgrad, bout, dwz, dwf, lines, sums, pay, gates = call(
         functools.partial(unattend_kernel, g), "unattend",
         (
-            hgrad, h1, qkv, lse, gat, wi, wix, small, mpart, dwf, mod, att, res, wof, gath, out_cotangent, rbias, ebs,
-            gates,
+            hgrad, h1, qkv, lse, gat, wi, wix, small, mpart, dwf, mod, att, res,
+            wof.reshape(T * g.hw, W), gath, out_cotangent, rbias, ebs, gates,
         ),
-        "vvvvvvvvhhvvvvvhvvv",
+        "vhhvvhhvhhvvvhhhvvv",
         [
-            ((g.Ro, W), F32), ((g.Ro, W), F32), ((g.Ro, W), BF), ((2 * g.units, g.zr, W), BF),
-            ((2 * g.units, ru, W), BF), ((8, W), F32), ((8, W), F32), ((2, 8, W), F32), ((2, 8, 128), F32),
+            ((g.Ro, W), F32), ((g.Ro, W), F32), ((g.Ro, W), BF), ((g.units, g.zr, W), BF),
+            ((g.units, g.fr, W), BF), ((8, W), F32), ((8, W), F32), ((2, 8, W), F32), ((2, 8, 128), F32),
         ],
         "vvvvvvvvv",
         [
+            V((g.Rc, W), BF), V((wide * 3, g.hd, g.Rc), BF), V((3 * g.hw, W), BF), V((3 * g.hw, W), BF),
+            V((G, g.Ro, W), BF), V((T * g.hw, W), BF), V((T * g.hw, g.Ro), BF),
             V((T, g.hw, g.Ro), BF), V((G, 2, g.hw, g.Ro), BF), V((T, g.hw, W), BF), V((G, g.hw, W), BF),
             V((G, g.hw, W), BF), V((8, W), F32),
             V((2, 3 * g.hw, g.L), BF), V((2, 3 * g.hw, W), F32), V((g.Ro, W), F32), V((G - 1, g.Ro, W), BF),
-            V((G - 1, g.Ro, W), BF), V((G, g.Ro, W), BF), V((3 * g.hw, W), BF), V((3 * g.hw, W), BF),
+            V((3 * g.hw, W), BF), V((3 * g.hw, W), BF),
             V((G - 1, g.hw, W), BF), V((T, 8, W), F32), V((g.Ro, W), BF),
         ]
-        + GroupSum.scratch(g, ru)
+        + GroupSum.scratch(g, g.units, g.fr)
+        + FirstLeg.scratch(g, g.ze, g.zr)
+        + PlaneScatter.scratch(g)
+        + PlaneScatter.scratch(g)
         + [
-            dma((G,)), dma((G,)), dma((G,)), dma((G,)), dma((G,)), dma((G,)), dma((T,)), dma((T,)), dma, dma,
-            dma((G,)), dma((G,)), dma((G,)), dma((G,)), dma((3,)),
+            dma((G,)), dma((G,)), dma((T,)), dma((T,)), dma, dma,
+            dma((G,)), dma((G,)), dma((G,)), dma((G,)), dma((9,)),
         ],
         4,
     )
@@ -1039,16 +1262,16 @@
         (grad, rgrad, tokens, mod, lines, sums, bout, pay, gates, dsg, dwz), "vvhvvvvvvvv",
         [
             ((g.R, W), BF), ((g.R, W), BF), ((D, T, 8, g.cw), F32), ((D, 8, W), F32), ((D, I, 128), F32),
-            ((2 * g.units, g.zr, W), BF),
+            ((g.units, g.zr, W), BF),
         ],
         "hhvvvv",
         [
             V((g.Ro, W), BF), V((g.Ro, W), BF), V((T, 8, g.cw), F32), V((D, T, 8, g.cw), F32), V((D, 8, W), F32),
             V((D, I, 128), F32), V((8, W), F32), V((8, 128), F32),
         ]
-        + GroupSum.scratch(g, g.zr)
+        + GroupSum.scratch(g, g.units, g.zr)
         + [
-            dma, dma((2, G)), dma((2, G)), dma((2, G)), dma((2, G)), dma((T,)), dma((T,)), dma((2,)), dma((2,)),
+            dma, dma((2, G, 2)), dma((2, G, 2)), dma((2, G)), dma((2, G)), dma((T,)), dma((T,)), dma((2,)), dma((2,)),
             dma((3, D)), dma((3, D)), dma((2,)),
         ],
         5,

time: 304 us -> 260 us (0.86)
  Pallas kernels: 281 us -> 237 us
    pallas_call x6, Pallas kernels: 281 us -> 237 us  [call(): pl.pallas_call(kernel, name=name, out_shape=[jax.ShapeDtypeStruct(s, t) f...]
where the time goes in v2:
time: 260 us; the launch traced here: 259 us
  Pallas kernels  237 us (91%)
  other arithmetic  11.2 us (4%)
  local copies, waits for them, and re-layouts  10.6 us (4%)
    pallas_call x6, Pallas kernels, call(): pl.pallas_call(kernel, name=name, out_shape=[jax.ShapeDtypeStruct(s, t) f...  237 us
    convert_element_type x1, other arithmetic, body(): ball.astype(F32)  6.84 us

profile of v2, /device:TPU:0, one launch (start us, length us, event | category | flops | bytes accessed | tf_op | source)
XLA Modules:
  0.0 259.0 jit_solution(9213467689170991313)
XLA Ops:
  0.6 1.3 reshape.57.eb
  1.9 0.0 copy-start.2
  1.9 14.6 %start.1 = (f32[6,8,1152]{2,1,0:T(8,128)}, f32[2,8,128]{2,1,0:T(8,128)}, f32[8,128]{1,0:T(8,128)}, f32[2,8,1152]{2,1,0:T(8,128)}, f32[4,8,1152]{2,1,0:T(8,128)},...) custom-call(f32[8,1152]{1,0:T(8,128)} %cond.1, bf16[864,1152]{1,0:T(8,128)(2,1)} %bitcast.32, ...), custom_call_target="tpu_custom_call" | custom-call | flops 100000000 | bytes 10000000 | tf_op jit(solution)/shard_map/start/pallas_call | solution.py:372
  16.5 0.0 copy-done.2
  16.5 0.6 reshape.58.ob
  17.1 31.1 %attend.1 = (bf16[1024,1152]{1,0:T(8,128)(2,1)}, bf16[12,72,1024]{2,1,0:T(8,128)(2,1)}, f32[4,1024]{1,0:T(4,128)}, f32[256,1152]{1,0:T(8,128)}, f32[256,1152]{1,...) custom-call(bf16[2048,1152]{1,0:T(8,128)(2,1)} %tokens.3, ...), custom_call_target="tpu_custom_call" | custom-call | flops 100000000 | bytes 10000000 | tf_op jit(solution)/shard_map/attend/pallas_call | solution.py:372
  48.2 0.0 copy-start.3
  48.2 50.9 %feed.1 = (f32[256,1152]{1,0:T(8,128)}, bf16[4,256,1152]{2,1,0:T(8,128)(2,1)}, bf16[8,144,1152]{2,1,0:T(8,128)(2,1)}, f32[8,1152]{1,0:T(8,128)}, f32[2,8,128]{2,1,0:T(8,128)}, /*index=5*/f32[2,8,1152]{2,1,0:T(8,128)}) custom-call(bf16[256,1152]{1,0:T(8,128)(2,1)} %get-tuple-element.61.h2, bf16[2048,1152]{1,0:T(8,128)(2,1)} %cotangent.3, ...), custom_call_target="tpu_custom_call" | custom-call | flops 100000000 | bytes 10000000 | tf_op jit(solution)/shard_map/feed/pallas_call | solution.py:372
  99.1 0.0 copy-done.3
  99.1 0.6 reshape.59.rbias
  99.7 85.5 %unattend.1 = (f32[256,1152]{1,0:T(8,128)}, f32[256,1152]{1,0:T(8,128)}, bf16[256,1152]{1,0:T(8,128)(2,1)}, bf16[8,72,1152]{2,1,0:T(8,128)(2,1)}, bf16[8,144,115...) custom-call(f32[256,1152]{1,0:T(8,128)} %get-tuple-element.64.hgrad,, ...), custom_call_target="tpu_custom_call" | custom-call | flops 100000000 | bytes 10000000 | tf_op jit(solution)/shard_map/unattend/pallas_call | solution.py:372
  185.2 50.3 %finish.1 = (bf16[2048,1152]{1,0:T(8,128)(2,1)}, bf16[2048,1152]{1,0:T(8,128)(2,1)}, f32[4,8,8,256]{3,2,1,0:T(8,128)}, f32[4,8,1152]{2,1,0:T(8,128)}, f32[4,8,12...) custom-call(f32[256,1152]{1,0:T(8,128)} %get-tuple-element.77.grad, f32[256,1152]{1,0:T(8,128)} %get-tuple-element.78.rgrad, ...), custom_call_target="tpu_custom_call" | custom-call | flops 100000000 | bytes 10000000 | tf_op jit(solution)/shard_map/finish/pallas_call | solution.py:372
  235.5 0.0 slice-start
  235.5 4.2 %wrap.1 = (f32[864,1152]{1,0:T(8,128)}, f32[6,144]{1,0:T(8,128)}, f32[2,2,1152]{2,1,0:T(2,128)}, f32[2,2]{1,0:T(2,128)}, f32[2,144]{1,0:T(2,128)}, /*index=5*/f32[8,1152]{1,0:T(8,128)}) custom-call(f32[4,8,8,256]{3,2,1,0:T(8,128)} %get-tuple-element.88.colall, f32[4,8,1152]{2,1,0:T(8,128)} %get-tuple-element.89.zall, f32[4,8,128]{2,1,0:T(8,128)} %get-tuple-element.90.logall, ...), custom_call_target="tpu_custom_call" | custom-call | flops 100000000 | bytes 10000000 | tf_op jit(solution)/shard_map/wrap/pallas_call | solution.py:372
  239.7 1.5 slice_reduce_fusion
  241.2 1.3 slice_reduce_fusion.2
  242.5 0.0 slice-start.1
  242.5 6.8 %convert_element_type.15 = f32[2048,1152]{1,0:T(8,128)} convert(bf16[2048,1152]{1,0:T(8,128)(2,1)} %get-tuple-element.86) | non-fusion elementwise | flops 2359296 | bytes 14155776 | tf_op jit(solution)/shard_map/convert_element_type | solution.py:1290
  249.4 0.0 slice-done
  249.4 0.0 slice-done.1
  249.4 0.0 copy-start.1
  249.4 4.4 %convert_element_type.16 = f32[2048,1152]{1,0:T(8,128)} convert(bf16[2048,1152]{1,0:T(8,128)(2,1)S(1)} %bitcast.28) | non-fusion elementwise | flops 2359296 | bytes 14155776 | tf_op jit(solution)/shard_map/convert_element_type | solution.py:1291
  253.7 0.0 copy-done.1
  253.7 0.0 copy-start
  253.7 1.4 slice.35
  255.1 0.9 slice.36
  256.0 0.3 copy-done
  256.3 2.7 %fusion = (f32[4,144,1152]{2,1,0:T(8,128)}, f32[4,144,1152]{2,1,0:T(8,128)}) fusion(bf16[8,144,1152]{2,1,0:T(8,128)(2,1)S(1)} %copy-done), kind=kLoop, calls=%fused_computation.3 | loop fusion | bytes 10616832 | tf_op jit(solution)/shard_map/slice | solution.py:1300
  (1 shorter events, 0.0 us)
Async XLA Ops:
  1.9 14.6 %copy-start.2 = (bf16[1152]{0:T(1024)(128)(2,1)S(1)}, bf16[1152]{0:T(1024)(128)(2,1)}, u32[]{:S(2)}) copy-start(bf16[1152]{0:T(1024)(128)(2,1)} %param.26) | copy-start | bytes 6916
  48.2 50.9 %copy-start.3 = (bf16[1152]{0:T(1024)(128)(2,1)S(1)}, bf16[1152]{0:T(1024)(128)(2,1)}, u32[]{:S(2)}) copy-start(bf16[1152]{0:T(1024)(128)(2,1)} %param.30) | copy-start | bytes 6916
  235.5 13.9 %slice-start = ((s8[4718592]{0:T(1024)(128)(4,1)}), s8[524288]{0:T(1024)(128)(4,1)S(1)}, s32[]{:S(2)}) async-start(s8[4718592]{0:T(1024)(128)(4,1)} %bitcast.27), calls=%async_computation | async-start | bytes 1048576
  242.5 6.8 %slice-start.1 = ((s8[4718592]{0:T(1024)(128)(4,1)}), s8[4194304]{0:T(1024)(128)(4,1)S(1)}, s32[]{:S(2)}) async-start(s8[4718592]{0:T(1024)(128)(4,1)} %bitcast.27), calls=%async_computation.1 | async-start | bytes 8388608
  249.4 4.4 %copy-start.1 = (bf16[8,72,1152]{2,1,0:T(8,128)(2,1)S(1)}, bf16[8,72,1152]{2,1,0:T(8,128)(2,1)}, u32[]{:S(2)}) copy-start(bf16[8,72,1152]{2,1,0:T(8,128)(2,1)} %get-tuple-element.94) | copy-start | bytes 3981316
  253.7 2.6 copy-start

commit v3 on v2

--- a/solution.py
+++ b/solution.py
@@ -85,11 +85,15 @@
         return d, t, t // 2, lax.rem(t, 2)
 
 
-def meet(devices):
+def greet(devices):
     barrier = pltpu.get_barrier_semaphore()
     for device in devices:
         pl.semaphore_signal(barrier, inc=1, device_id=device, device_id_type=MESH)
-    pl.semaphore_wait(barrier, len(devices))
+    return barrier
+
+
+def meet(devices):
+    pl.semaphore_wait(greet(devices), len(devices))
 
 
 def meet_line(g, devices, group, middle):
@@ -384,21 +388,15 @@
 
 
 def start_kernel(
-    g, cond, wm, mb, ts, masks, rw, rb, eb, ib, wi, we, wr,
-    mod, gat, dsg, smc, call_all, wix, wex, wrx,
+    g, cond, wm, mb, ts, masks, rw, rb, eb, ib, wi,
+    mod, gat, dsg, smc, call_all, wix,
     mpart, gx, sx, cx, send_m, recv_m, send_w, recv_w, send_c, recv_c,
 ):
     d, t, p, c = g.place()
     partner = (d, p * 2 + 1 - c)
-    meet(
-        [(d, flip(t, k, g.tbits)) for k in range(1, g.T)] + [(flip(d, k, g.dbits), t) for k in range(1, g.D)]
-    )
-    pair = [
-        remote(src, dst, send_w.at[index], recv_w.at[index], partner)
-        for index, (src, dst) in enumerate(((wi, wix), (we, wex), (wr, wrx)))
-    ]
-    for copy in pair:
-        copy.start()
+    devices = [(d, flip(t, k, g.tbits)) for k in range(1, g.T)]
+    devices = devices + [(flip(d, k, g.dbits), t) for k in range(1, g.D)]
+    barrier = greet(devices)
     value = cond[...]
     silu = (value / (1.0 + jnp.exp(-value))).astype(BF)
     part = nt(silu, wm[...])
@@ -407,6 +405,9 @@
     for row in range(6):
         mpart[t, :, row * w : (row + 1) * w] = part[:, row * w : (row + 1) * w] + bias[row : row + 1]
 
+    pl.semaphore_wait(barrier, len(devices))
+    pair = remote(wi, wix, send_w.at[2], recv_w.at[2], partner)
+
     def spread(k):
         return remote(
             mpart.at[t], mpart.at[t], send_m.at[k], recv_m.at[k], (d, flip(t, k, g.tbits))
@@ -414,6 +415,7 @@
 
     for k in range(1, g.T):
         spread(k).start()
+    pair.start()
     low = value.astype(BF)
     steps = masks.shape[2]
     row = lax.broadcasted_iota(jnp.int32, (g.I, steps), 0)
@@ -434,8 +436,8 @@
     sx[0, 0:1, : g.ch] = eb[...]
     sx[0, 1:3, : g.hw] = ib[...].astype(F32)
     small = [
-        remote(gx.at[0], gx.at[1], send_w.at[3], recv_w.at[3], partner),
-        remote(sx.at[0], sx.at[1], send_w.at[4], recv_w.at[4], partner),
+        remote(gx.at[0], gx.at[1], send_w.at[0], recv_w.at[0], partner),
+        remote(sx.at[0], sx.at[1], send_w.at[1], recv_w.at[1], partner),
     ]
     for copy in small:
         copy.start()
@@ -455,8 +457,7 @@
         copy.wait()
     gat[...] = gx[...]
     smc[...] = sx[...]
-    for copy in pair:
-        copy.wait()
+    pair.wait()
     for k in range(1, g.D):
         conditions(k).wait()
     call_all[...] = cx[...]
@@ -467,9 +468,9 @@
 
 
 def attend_kernel(
-    g, tokens, mod, gat, smc, wi, wix, wo, ob,
-    h1_out, qkv_out, lse, att, res, h2, gath, wof,
-    tok, h1, qkv, gsend, gbuf, wob, load, keep, save, send, recv, send_o, recv_o, send_f, recv_f,
+    g, tokens, mod, gat, smc, wi, wix, wo, ob, we, wr,
+    h1_out, qkv_out, lse, att, res, h2, gath, wof, wex, wrx,
+    tok, h1, qkv, gsend, gbuf, wob, bias, send_w, recv_w, load, keep, save, send, recv, send_o, recv_o, send_f, recv_f,
 ):
     d, t, p, c = g.place()
     partner = (d, p * 2 + 1 - c)
@@ -489,10 +490,22 @@
     for k in range(1, g.G):
         share(k).start()
     forward(0).start()
+    pair = [
+        remote(src, dst, send_w.at[index], recv_w.at[index], partner)
+        for index, (src, dst) in enumerate(((we, wex), (wr, wrx)))
+    ]
+    for weight in pair:
+        weight.start()
     wob[t] = wo[...]
     copy.wait()
     scale = 1.0 / math.sqrt(g.hd)
     ones = jnp.ones((8, g.L), BF)
+    for s in range(2):
+        for r in range(2):
+            line = jnp.where(
+                lax.broadcasted_iota(jnp.int32, (8, g.hw), 0) == r + 1, smc[s, :, : g.hw], 0.0
+            )
+            bias[s, r] = tn(line.astype(BF), ones)
 
     def chunk(j):
         i, u = j // g.sub, lax.rem(j, g.sub)
@@ -532,17 +545,12 @@
             wide = nt(weights[s][...], hidden)
             core = c + s - 2 * c * s
             parts = split_heads(g, wide)
-            rowsum = smc[s].astype(BF)
-            bias = []
-            for r in (1, 2):
-                line = jnp.where(lax.broadcasted_iota(jnp.int32, (8, g.hw), 0) == r, rowsum[:, : g.hw].astype(F32), 0.0)
-                bias.append(tn(line.astype(BF), ones))
             for h in range(g.lh):
                 hh = s * g.lh + h
                 rows_h = slice(h * g.hd, (h + 1) * g.hd)
-                q = (parts[h] + bias[0][rows_h]).astype(BF)
+                q = (parts[h] + bias[s, 0, rows_h]).astype(BF)
                 k = parts[g.lh + h].astype(BF)
-                v = (parts[2 * g.lh + h] + bias[1][rows_h]).astype(BF)
+                v = (parts[2 * g.lh + h] + bias[s, 1, rows_h]).astype(BF)
                 qkv[hh * 3 + 0, :, rows] = q
                 qkv[hh * 3 + 1, :, rows] = k
                 qkv[hh * 3 + 2, :, rows] = v
@@ -596,6 +604,8 @@
     for k in range(g.G):
         forward(k).wait_send()
     for copy in saves:
+        copy.wait()
+    for copy in pair:
         copy.wait()
 
 
@@ -1120,38 +1130,107 @@
             arrive_forward(which, dst, k).wait_recv()
 
 
-def wrap_kernel(g, colall, zall, logall, conds, dwm, dmb, drw, drb, dib, vectors):
-    rows = []
-    for member in range(g.T):
-        rows.append(((member % 2) * g.G + member // 2) * g.Ro // g.L)
-    value = conds[...]
-    silu = value / (1.0 + jnp.exp(-value))
-    picked = jnp.concatenate([silu[z, i : i + 1] for z in range(g.D) for i in rows], axis=0).astype(BF)
-    twice = jnp.concatenate([picked, picked], axis=0)
+def wrap_kernel(
+    g, ball, tall, dwf, dwz, colall, zall, logall, conds,
+    out, tokens_grad, dwr, dwe, dwi, dwo, dwm, dmb, drw, drb, dib, deb, dob, drb_all,
+    twice,
+):
+    step = pl.program_id(0)
+    out[...] = ball[...].astype(F32)
+    tokens_grad[...] = tall[...].astype(F32)
+    half_units = g.units // 2
+    heads = 3 * g.units // 4
+
+    @pl.when(step < half_units)
+    def _():
+        dwr[...] = dwf[...].astype(F32)
+
+    @pl.when(step >= half_units)
+    def _():
+        dwe[...] = dwf[...].astype(F32)
+
+    @pl.when(step < heads)
+    def _():
+        dwi[...] = dwz[...].astype(F32)
+
+    @pl.when(step >= heads)
+    def _():
+        dwo[...] = dwz[...].astype(F32)
+
     w = g.mw
-    for row in range(6):
+
+    @pl.when(step == 0)
+    def _():
+        rows = []
+        for member in range(g.T):
+            rows.append(((member % 2) * g.G + member // 2) * g.Ro // g.L)
+        value = conds[...]
+        silu = value / (1.0 + jnp.exp(-value))
+        picked = jnp.concatenate([silu[z, i : i + 1] for z in range(g.D) for i in rows], axis=0).astype(BF)
+        twice[...] = jnp.concatenate([picked, picked], axis=0)
+        logits = jnp.concatenate([logall[z] for z in range(g.D)], axis=0)
+        high = logits.astype(BF)
+        low = (logits - high.astype(F32)).astype(BF)
+        flat = jnp.concatenate([value[z] for z in range(g.D)], axis=0).astype(BF)
+        router = tn(jnp.concatenate([high, low], axis=0), jnp.concatenate([flat, flat], axis=0))
+        sums = jnp.sum(logits, axis=0, keepdims=True)
+        for h in range(g.lh):
+            drw[h] = router[2 * h : 2 * h + 2, :]
+            drb[h : h + 1, :] = sums[:, 2 * h : 2 * h + 2]
+        total = zall[0]
+        for z in range(1, g.D):
+            total = total + zall[z]
+        dib[0:1, :] = total[1:2, : g.hw]
+        dib[1:2, :] = total[1:2, 2 * g.hw : 3 * g.hw]
+        deb[...] = total[0, : g.ch]
+        dob[...] = total[2]
+        drb_all[...] = total[3]
+
+    @pl.when(step < 6)
+    def _():
         part = jnp.concatenate(
-            [colall[z, member, row : row + 1, :] for z in range(g.D) for member in range(g.T)], axis=0
+            [colall[z, member, pl.ds(step, 1), :] for z in range(g.D) for member in range(g.T)], axis=0
         )
-        dmb[row : row + 1, :] = jnp.sum(part, axis=0, keepdims=True)[:, :w]
+        dmb[pl.ds(step, 1), :] = jnp.sum(part, axis=0, keepdims=True)[:, :w]
         high = part.astype(BF)
         low = (part - high.astype(F32)).astype(BF)
-        dwm[row * w : (row + 1) * w, :] = tn(jnp.concatenate([high, low], axis=0), twice)[:w]
-    logits = jnp.concatenate([logall[z] for z in range(g.D)], axis=0)
-    high = logits.astype(BF)
-    low = (logits - high.astype(F32)).astype(BF)
-    flat = jnp.concatenate([value[z] for z in range(g.D)], axis=0).astype(BF)
-    router = tn(jnp.concatenate([high, low], axis=0), jnp.concatenate([flat, flat], axis=0))
-    sums = jnp.sum(logits, axis=0, keepdims=True)
-    for h in range(g.lh):
-        drw[h] = router[2 * h : 2 * h + 2, :]
-        drb[h : h + 1, :] = sums[:, 2 * h : 2 * h + 2]
-    total = zall[0]
-    for z in range(1, g.D):
-        total = total + zall[z]
-    dib[0:1, :] = total[1:2, : g.hw]
-    dib[1:2, :] = total[1:2, 2 * g.hw : 3 * g.hw]
-    vectors[...] = total
+        dwm[...] = tn(jnp.concatenate([high, low], axis=0), twice[...])[:w]
+
+
+def wrap(g, ball, tall, dwf, dwz, colall, zall, logall, conds):
+    n, W = g.units, g.W
+    half_units, heads = n // 2, 3 * n // 4
+    rows = g.R // n
+
+    def whole(shape):
+        return pl.BlockSpec(shape, lambda i: (0,) * len(shape))
+
+    def part(shape, low, count):
+        return pl.BlockSpec(shape, lambda i: (jnp.clip(i - low, 0, count - 1),) + (0,) * (len(shape) - 1))
+
+    outs = [
+        ((g.R, W), part((rows, W), 0, n)), ((g.R, W), part((rows, W), 0, n)),
+        ((half_units, g.fr, W), part((1, g.fr, W), 0, half_units)),
+        ((half_units, g.fr, W), part((1, g.fr, W), half_units, half_units)),
+        ((heads, g.zr, W), part((1, g.zr, W), 0, heads)), ((n - heads, g.zr, W), part((1, g.zr, W), heads, n - heads)),
+        ((6 * g.mw, W), part((g.mw, W), 0, 6)), ((6, g.mw), whole((6, g.mw))), ((g.lh, 2, W), whole((g.lh, 2, W))),
+        ((g.lh, 2), whole((g.lh, 2))), ((2, g.hw), whole((2, g.hw))), ((g.ch,), whole((g.ch,))), ((W,), whole((W,))),
+        ((W,), whole((W,))),
+    ]
+    return pl.pallas_call(
+        functools.partial(wrap_kernel, g),
+        name="wrap",
+        grid=(n,),
+        out_shape=[jax.ShapeDtypeStruct(s, F32) for s, _ in outs],
+        in_specs=[
+            part((rows, W), 0, n), part((rows, W), 0, n), part((1, g.fr, W), 0, n), part((1, g.zr, W), 0, n),
+            whole(colall.shape), whole(zall.shape), whole(logall.shape), whole(conds.shape),
+        ],
+        out_specs=[spec for _, spec in outs],
+        scratch_shapes=[pltpu.VMEM((2 * g.D * g.T, W), BF)],
+        cost_estimate=pl.CostEstimate(flops=10**9, bytes_accessed=4 * 10**7, transcendentals=0),
+        compiler_params=pltpu.CompilerParams(vmem_limit_bytes=VMEM_LIMIT),
+    )(ball, tall, dwf, dwz, colall, zall, logall, conds)
 
 
 def body(
@@ -1178,32 +1257,33 @@
     ob = output_bias.astype(F32)[None]
     rbias = reduce_bias.astype(F32)[None]
 
-    mod, gat, dsg, smc, conds, wix, wex, wrx = call(
+    mod, gat, dsg, smc, conds, wix = call(
         functools.partial(start_kernel, g), "start",
-        (condition, wm, modulate_bias, timesteps, masks, rw, router_bias, eb, input_bias, wi, we, wr),
-        "vvvsvvvvvhhh",
+        (condition, wm, modulate_bias, timesteps, masks, rw, router_bias, eb, input_bias, wi),
+        "vvvsvvvvvh",
         [
             ((6, I, W), F32), ((2, I, 128), F32), ((I, 128), F32), ((2, 8, W), F32), ((D, I, W), F32),
-            ((3 * g.hw, W), BF), ((g.ch, W), BF), ((g.ch, W), BF),
+            ((3 * g.hw, W), BF),
         ],
-        "vvvvvhhh",
+        "vvvvvh",
         [
             V((T, I, 6 * g.mw), F32), V((2, I, 128), F32), V((2, 8, W), F32), V((D, I, W), F32),
-            dma((T,)), dma((T,)), dma((5,)), dma((5,)), dma((D,)), dma((D,)),
+            dma((T,)), dma((T,)), dma((3,)), dma((3,)), dma((D,)), dma((D,)),
         ],
         1,
     )
-    h1, qkv, lse, att, res, h2, gath, wof = call(
+    h1, qkv, lse, att, res, h2, gath, wof, wex, wrx = call(
         functools.partial(attend_kernel, g), "attend",
-        (tokens, mod, gat, smc, wi, wix, output_weight, ob), "hvvvvvvv",
+        (tokens, mod, gat, smc, wi, wix, output_weight, ob, we, wr), "hvvvvvvvhh",
         [
             ((g.Rc, W), BF), ((wide * 3, g.hd, g.Rc), BF), ((wide, g.Rc), F32),
             ((g.Ro, W), F32), ((g.Ro, W), F32), ((g.Ro, W), BF), ((T * g.hw, g.Ro), BF), ((T, g.hw, W), BF),
+            ((g.ch, W), BF), ((g.ch, W), BF),
         ],
-        "hhvvvvvh",
+        "hhvvvvvhhh",
         [
             V((g.Rc, W), BF), V((g.Rc, W), BF), V((wide * 3, g.hd, g.Rc), BF), V((g.Ic, 2, g.hw, g.L), BF), V((T, g.hw, g.Ro), BF), V((T, g.hw, W), BF),
-            dma, dma, dma((3,)), dma((G,)), dma((G,)), dma((G,)), dma((G,)), dma((G,)), dma((G,)),
+            V((2, 2, g.hw, g.L), F32), dma((2,)), dma((2,)), dma, dma, dma((3,)), dma((G,)), dma((G,)), dma((G,)), dma((G,)), dma((G,)), dma((G,)),
         ],
         2,
     )
@@ -1276,29 +1356,22 @@
         ],
         5,
     )
-    dwm, dmb, drw, drb, dib, vectors = call(
-        functools.partial(wrap_kernel, g), "wrap", (colall, zall, logall, conds), "vvvv",
-        [
-            ((6 * g.mw, W), F32), ((6, g.mw), F32), ((g.lh, 2, W), F32), ((g.lh, 2), F32), ((2, g.hw), F32),
-            ((8, W), F32),
-        ],
-        "vvvvvv", [], None,
+    out, tokens_grad, dwr, dwe, dwi, dwo, dwm, dmb, drw, drb, dib, deb, dob, drb_all = wrap(
+        g, ball, tall, dwf, dwz, colall, zall, logall, conds
     )
-    dwf = dwf.astype(F32).reshape(2, g.ch, W)
-    dwz = dwz.astype(F32).reshape(4 * g.hw, W)
     return (
-        ball.astype(F32),
-        tall.astype(F32),
+        out,
+        tokens_grad,
         jnp.transpose(dwm.reshape(6, g.mw, W), (2, 0, 1)),
         dmb,
-        jnp.transpose(dwz[: 3 * g.hw].reshape(3, g.hw, W), (2, 0, 1)),
+        jnp.transpose(dwi.reshape(3, g.hw, W), (2, 0, 1)),
         dib,
-        dwz[3 * g.hw :],
-        vectors[2],
-        dwf[1].T,
-        vectors[0, : g.ch],
-        dwf[0],
-        vectors[3],
+        dwo.reshape(g.hw, W),
+        dob,
+        dwe.reshape(g.ch, W).T,
+        deb,
+        dwr.reshape(g.ch, W),
+        drb_all,
         jnp.transpose(drw, (2, 0, 1)),
         drb,
     )

time: 260 us -> 253 us (0.973)
  other arithmetic: 11.2 us -> 0 us
  Pallas kernels: 237 us -> 247 us
  local copies, waits for them, and re-layouts: 10.6 us -> 3.83 us
    pallas_call x0 -> x1, Pallas kernels: none -> 17.3 us  [wrap(): pl.pallas_call(functools.partial(wrap_kernel, g), name='wrap', grid=(n,),...]
    convert_element_type x2 -> x0, other arithmetic: 11.2 us -> none  [the longest x1 6.84 us: body(): ball.astype(F32)]
    slice x5 -> x0, local copies, waits for them, and re-layouts: 7.82 us -> none  [the longest x1 2.72 us: body(): dwf[0]]
    pallas_call x6 -> x5, Pallas kernels: 237 us -> 230 us  [call(): pl.pallas_call(kernel, name=name, out_shape=[jax.ShapeDtypeStruct(s, t) f...]
where the time goes in v3:
time: 253 us; the launch traced here: 252 us
  Pallas kernels  247 us (98%)
  local copies, waits for them, and re-layouts  3.83 us (2%)
    pallas_call x5, Pallas kernels, call(): pl.pallas_call(kernel, name=name, out_shape=[jax.ShapeDtypeStruct(s, t) f...  230 us
    pallas_call x1, Pallas kernels, wrap(): pl.pallas_call(functools.partial(wrap_kernel, g), name='wrap', grid=(n,),...  17.3 us

profile of v3, /device:TPU:0, one launch (start us, length us, event | category | flops | bytes accessed | tf_op | source)
XLA Modules:
  0.0 251.9 jit_solution(13976859223207492284)
XLA Ops:
  0.6 1.3 reshape.60.eb
  1.9 1.3 reshape.61.ob
  3.2 1.3 reshape.62.rbias
  4.5 13.8 %start.1 = (f32[6,8,1152]{2,1,0:T(8,128)}, f32[2,8,128]{2,1,0:T(8,128)}, f32[8,128]{1,0:T(8,128)}, f32[2,8,1152]{2,1,0:T(8,128)}, f32[4,8,1152]{2,1,0:T(8,128)}, /*index=5*/bf16[432,1152]{1,0:T(8,128)(2,1)}) custom-call(f32[8,1152]{1,0:T(8,128)} %cond.1, bf16[864,1152]{1,0:T(8,128)(2,1)} %bitcast.28, bf16[6,144]{1,0:T(8,128)(2,1)} %mb.1, s32[8]{0:T(128)} %ts.1, ...), custom_call_target="tpu_custom_call" | custom-call | flops 100000000 | bytes 10000000 | tf_op jit(solution)/shard_map/start/pallas_call | solution.py:376
  18.3 28.6 %attend.1 = (bf16[1024,1152]{1,0:T(8,128)(2,1)}, bf16[12,72,1024]{2,1,0:T(8,128)(2,1)}, f32[4,1024]{1,0:T(4,128)}, f32[256,1152]{1,0:T(8,128)}, f32[256,1152]{1,...) custom-call(bf16[2048,1152]{1,0:T(8,128)(2,1)} %tokens.3, ...), custom_call_target="tpu_custom_call" | custom-call | flops 100000000 | bytes 10000000 | tf_op jit(solution)/shard_map/attend/pallas_call | solution.py:376
  47.0 51.9 %feed.1 = (f32[256,1152]{1,0:T(8,128)}, bf16[4,256,1152]{2,1,0:T(8,128)(2,1)}, bf16[8,144,1152]{2,1,0:T(8,128)(2,1)}, f32[8,1152]{1,0:T(8,128)}, f32[2,8,128]{2,1,0:T(8,128)}, /*index=5*/f32[2,8,1152]{2,1,0:T(8,128)}) custom-call(bf16[256,1152]{1,0:T(8,128)(2,1)} %get-tuple-element.69.h2, bf16[2048,1152]{1,0:T(8,128)(2,1)} %cotangent.3, ...), custom_call_target="tpu_custom_call" | custom-call | flops 100000000 | bytes 10000000 | tf_op jit(solution)/shard_map/feed/pallas_call | solution.py:376
  98.9 84.6 %unattend.1 = (f32[256,1152]{1,0:T(8,128)}, f32[256,1152]{1,0:T(8,128)}, bf16[256,1152]{1,0:T(8,128)(2,1)}, bf16[8,72,1152]{2,1,0:T(8,128)(2,1)}, bf16[8,144,115...) custom-call(f32[256,1152]{1,0:T(8,128)} %get-tuple-element.72.hgrad,, ...), custom_call_target="tpu_custom_call" | custom-call | flops 100000000 | bytes 10000000 | tf_op jit(solution)/shard_map/unattend/pallas_call | solution.py:376
  183.5 50.9 %finish.1 = (bf16[2048,1152]{1,0:T(8,128)(2,1)}, bf16[2048,1152]{1,0:T(8,128)(2,1)}, f32[4,8,8,256]{3,2,1,0:T(8,128)}, f32[4,8,1152]{2,1,0:T(8,128)}, f32[4,8,12...) custom-call(f32[256,1152]{1,0:T(8,128)} %get-tuple-element.85.grad, f32[256,1152]{1,0:T(8,128)} %get-tuple-element.86.rgrad, ...), custom_call_target="tpu_custom_call" | custom-call | flops 100000000 | bytes 10000000 | tf_op jit(solution)/shard_map/finish/pallas_call | solution.py:376
  234.4 17.3 %wrap.1 = (f32[2048,1152]{1,0:T(8,128)}, f32[2048,1152]{1,0:T(8,128)}, f32[4,144,1152]{2,1,0:T(8,128)}, f32[4,144,1152]{2,1,0:T(8,128)}, f32[6,72,1152]{2,1,0:T(...) custom-call(bf16[2048,1152]{1,0:T(8,128)(2,1)} %get-tuple-element.94, ...), custom_call_target="tpu_custom_call" | custom-call | flops 1000000000 | bytes 40000000 | tf_op jit(solution)/shard_map/wrap/pallas_call | solution.py:1220

commit v4 on v3

--- a/solution.py
+++ b/solution.py
@@ -433,7 +433,7 @@
         dsg[:, 2 * h : 2 * h + 2] = mask * sigmoid * (1.0 - sigmoid)
         gx[0, :, 2 * h : 2 * h + 2] = mask * sigmoid
     sx[0] = jnp.zeros((8, g.W), F32)
-    sx[0, 0:1, : g.ch] = eb[...]
+    sx[0, 0:1, : g.ch] = eb[...].astype(F32).reshape(1, g.ch)
     sx[0, 1:3, : g.hw] = ib[...].astype(F32)
     small = [
         remote(gx.at[0], gx.at[1], send_w.at[0], recv_w.at[0], partner),
@@ -590,7 +590,7 @@
     saves.append(pltpu.make_async_copy(wob, wof, save.at[2]))
     saves[-1].start()
     full = wob[...].reshape(g.T * g.hw, g.W)
-    attention = tn(heads, full) + ob[...]
+    attention = tn(heads, full) + ob[...].astype(F32).reshape(1, g.W)
     own = c * g.Ic + p // g.sub
     base = tok[pl.ds(pl.multiple_of(p * g.Ro, g.Ro), g.Ro)].astype(F32)
     residual = base + mod[2, pl.ds(own, 1), :] * attention
@@ -968,7 +968,7 @@
         if low >= 3 * g.hw:
             dwz[u] = out[low - 3 * g.hw : low - 3 * g.hw + g.zr].astype(BF)
     zsum.settle([6])
-    branch = on.total(mpart[0].astype(F32)) + rbias[...]
+    branch = on.total(mpart[0].astype(F32)) + rbias[...].astype(F32).reshape(1, g.W)
     bout[...] = (res[...] + mod[5, pl.ds(own, 1), :] * branch).astype(BF)
     lines[...] = small[...]
     lines[5:6, :] = jnp.sum(cot[...].astype(F32) * branch, axis=0, keepdims=True)
@@ -1253,9 +1253,7 @@
     wr = reduce_weight
     rw = jnp.transpose(router_weight, (1, 2, 0))
     masks = jnp.transpose(route_masks, (1, 2, 0))
-    eb = expand_bias.astype(F32)[None]
-    ob = output_bias.astype(F32)[None]
-    rbias = reduce_bias.astype(F32)[None]
+    eb, ob, rbias = expand_bias, output_bias, reduce_bias
 
     mod, gat, dsg, smc, conds, wix = call(
         functools.partial(start_kernel, g), "start",

time: 253 us -> 249 us (0.984)
  local copies, waits for them, and re-layouts: 3.83 us -> 0 us
    broadcast_in_dim x3 -> x0, local copies, waits for them, and re-layouts: 3.83 us -> none  [the longest x1 1.28 us: body(): ob = output_bias.astype(F32)[None]]
where the time goes in v4:
time: 249 us; the launch traced here: 248 us
  Pallas kernels  247 us (99%)
    pallas_call x5, Pallas kernels, call(): pl.pallas_call(kernel, name=name, out_shape=[jax.ShapeDtypeStruct(s, t) f...  230 us
    pallas_call x1, Pallas kernels, wrap(): pl.pallas_call(functools.partial(wrap_kernel, g), name='wrap', grid=(n,),...  17.3 us

profile of v4, /device:TPU:0, one launch (start us, length us, event | category | flops | bytes accessed | tf_op | source)
XLA Modules:
  0.0 248.1 jit_solution(10917071353798802078)
XLA Ops:
  0.6 13.8 %start.1 = (f32[6,8,1152]{2,1,0:T(8,128)}, f32[2,8,128]{2,1,0:T(8,128)}, f32[8,128]{1,0:T(8,128)}, f32[2,8,1152]{2,1,0:T(8,128)}, f32[4,8,1152]{2,1,0:T(8,128)}, /*index=5*/bf16[432,1152]{1,0:T(8,128)(2,1)}) custom-call(f32[8,1152]{1,0:T(8,128)} %cond.1, bf16[864,1152]{1,0:T(8,128)(2,1)} %bitcast.28, bf16[6,144]{1,0:T(8,128)(2,1)} %mb.1, s32[8]{0:T(128)} %ts.1, ...), custom_call_target="tpu_custom_call" | custom-call | flops 100000000 | bytes 10000000 | tf_op jit(solution)/shard_map/start/pallas_call | solution.py:376
  14.5 28.6 %attend.1 = (bf16[1024,1152]{1,0:T(8,128)(2,1)}, bf16[12,72,1024]{2,1,0:T(8,128)(2,1)}, f32[4,1024]{1,0:T(4,128)}, f32[256,1152]{1,0:T(8,128)}, f32[256,1152]{1,...) custom-call(bf16[2048,1152]{1,0:T(8,128)(2,1)} %tokens.3, ...), custom_call_target="tpu_custom_call" | custom-call | flops 100000000 | bytes 10000000 | tf_op jit(solution)/shard_map/attend/pallas_call | solution.py:376
  43.2 51.9 %feed.1 = (f32[256,1152]{1,0:T(8,128)}, bf16[4,256,1152]{2,1,0:T(8,128)(2,1)}, bf16[8,144,1152]{2,1,0:T(8,128)(2,1)}, f32[8,1152]{1,0:T(8,128)}, f32[2,8,128]{2,1,0:T(8,128)}, /*index=5*/f32[2,8,1152]{2,1,0:T(8,128)}) custom-call(bf16[256,1152]{1,0:T(8,128)(2,1)} %get-tuple-element.69.h2, bf16[2048,1152]{1,0:T(8,128)(2,1)} %cotangent.3, ...), custom_call_target="tpu_custom_call" | custom-call | flops 100000000 | bytes 10000000 | tf_op jit(solution)/shard_map/feed/pallas_call | solution.py:376
  95.1 84.6 %unattend.1 = (f32[256,1152]{1,0:T(8,128)}, f32[256,1152]{1,0:T(8,128)}, bf16[256,1152]{1,0:T(8,128)(2,1)}, bf16[8,72,1152]{2,1,0:T(8,128)(2,1)}, bf16[8,144,115...) custom-call(f32[256,1152]{1,0:T(8,128)} %get-tuple-element.72.hgrad,, ...), custom_call_target="tpu_custom_call" | custom-call | flops 100000000 | bytes 10000000 | tf_op jit(solution)/shard_map/unattend/pallas_call | solution.py:376
  179.7 50.9 %finish.1 = (bf16[2048,1152]{1,0:T(8,128)(2,1)}, bf16[2048,1152]{1,0:T(8,128)(2,1)}, f32[4,8,8,256]{3,2,1,0:T(8,128)}, f32[4,8,1152]{2,1,0:T(8,128)}, f32[4,8,12...) custom-call(f32[256,1152]{1,0:T(8,128)} %get-tuple-element.85.grad, f32[256,1152]{1,0:T(8,128)} %get-tuple-element.86.rgrad, ...), custom_call_target="tpu_custom_call" | custom-call | flops 100000000 | bytes 10000000 | tf_op jit(solution)/shard_map/finish/pallas_call | solution.py:376
  230.6 17.3 %wrap.1 = (f32[2048,1152]{1,0:T(8,128)}, f32[2048,1152]{1,0:T(8,128)}, f32[4,144,1152]{2,1,0:T(8,128)}, f32[4,144,1152]{2,1,0:T(8,128)}, f32[6,72,1152]{2,1,0:T(...) custom-call(bf16[2048,1152]{1,0:T(8,128)(2,1)} %get-tuple-element.94, ...), custom_call_target="tpu_custom_call" | custom-call | flops 1000000000 | bytes 40000000 | tf_op jit(solution)/shard_map/wrap/pallas_call | solution.py:1220

commit v5 on v4

--- a/solution.py
+++ b/solution.py
@@ -972,10 +972,10 @@
     bout[...] = (res[...] + mod[5, pl.ds(own, 1), :] * branch).astype(BF)
     lines[...] = small[...]
     lines[5:6, :] = jnp.sum(cot[...].astype(F32) * branch, axis=0, keepdims=True)
+    zsum.settle([7])
     grad[...] = back.total(own_g[...])
     on.sent()
     back.sent()
-    zsum.settle([7])
     leg.add()
     zsum.end(everything, everything[g.fe :])
     leg.sent()

time: 249 us -> 244 us (0.980)
  Pallas kernels: 247 us -> 243 us
    pallas_call x5, Pallas kernels: 230 us -> 226 us  [call(): pl.pallas_call(kernel, name=name, out_shape=[jax.ShapeDtypeStruct(s, t) f...]
where the time goes in v5:
time: 244 us
  Pallas kernels  243 us (100%)
    pallas_call x5, Pallas kernels, call(): pl.pallas_call(kernel, name=name, out_shape=[jax.ShapeDtypeStruct(s, t) f...  226 us
    pallas_call x1, Pallas kernels, wrap(): pl.pallas_call(functools.partial(wrap_kernel, g), name='wrap', grid=(n,),...  17.3 us

profile of v5, /device:TPU:0, one launch (start us, length us, event | category | flops | bytes accessed | tf_op | source)
XLA Modules:
  0.0 243.8 jit_solution(10716726554916311414)
XLA Ops:
  0.6 13.8 %start.1 = (f32[6,8,1152]{2,1,0:T(8,128)}, f32[2,8,128]{2,1,0:T(8,128)}, f32[8,128]{1,0:T(8,128)}, f32[2,8,1152]{2,1,0:T(8,128)}, f32[4,8,1152]{2,1,0:T(8,128)}, /*index=5*/bf16[432,1152]{1,0:T(8,128)(2,1)}) custom-call(f32[8,1152]{1,0:T(8,128)} %cond.1, bf16[864,1152]{1,0:T(8,128)(2,1)} %bitcast.28, bf16[6,144]{1,0:T(8,128)(2,1)} %mb.1, s32[8]{0:T(128)} %ts.1, ...), custom_call_target="tpu_custom_call" | custom-call | flops 100000000 | bytes 10000000 | tf_op jit(solution)/shard_map/start/pallas_call | solution.py:376
  14.5 28.6 %attend.1 = (bf16[1024,1152]{1,0:T(8,128)(2,1)}, bf16[12,72,1024]{2,1,0:T(8,128)(2,1)}, f32[4,1024]{1,0:T(4,128)}, f32[256,1152]{1,0:T(8,128)}, f32[256,1152]{1,...) custom-call(bf16[2048,1152]{1,0:T(8,128)(2,1)} %tokens.3, ...), custom_call_target="tpu_custom_call" | custom-call | flops 100000000 | bytes 10000000 | tf_op jit(solution)/shard_map/attend/pallas_call | solution.py:376
  43.2 51.9 %feed.1 = (f32[256,1152]{1,0:T(8,128)}, bf16[4,256,1152]{2,1,0:T(8,128)(2,1)}, bf16[8,144,1152]{2,1,0:T(8,128)(2,1)}, f32[8,1152]{1,0:T(8,128)}, f32[2,8,128]{2,1,0:T(8,128)}, /*index=5*/f32[2,8,1152]{2,1,0:T(8,128)}) custom-call(bf16[256,1152]{1,0:T(8,128)(2,1)} %get-tuple-element.69.h2, bf16[2048,1152]{1,0:T(8,128)(2,1)} %cotangent.3, ...), custom_call_target="tpu_custom_call" | custom-call | flops 100000000 | bytes 10000000 | tf_op jit(solution)/shard_map/feed/pallas_call | solution.py:376
  95.1 80.0 %unattend.1 = (f32[256,1152]{1,0:T(8,128)}, f32[256,1152]{1,0:T(8,128)}, bf16[256,1152]{1,0:T(8,128)(2,1)}, bf16[8,72,1152]{2,1,0:T(8,128)(2,1)}, bf16[8,144,115...) custom-call(f32[256,1152]{1,0:T(8,128)} %get-tuple-element.72.hgrad,, ...), custom_call_target="tpu_custom_call" | custom-call | flops 100000000 | bytes 10000000 | tf_op jit(solution)/shard_map/unattend/pallas_call | solution.py:376
  175.1 51.2 %finish.1 = (bf16[2048,1152]{1,0:T(8,128)(2,1)}, bf16[2048,1152]{1,0:T(8,128)(2,1)}, f32[4,8,8,256]{3,2,1,0:T(8,128)}, f32[4,8,1152]{2,1,0:T(8,128)}, f32[4,8,12...) custom-call(f32[256,1152]{1,0:T(8,128)} %get-tuple-element.85.grad, f32[256,1152]{1,0:T(8,128)} %get-tuple-element.86.rgrad, ...), custom_call_target="tpu_custom_call" | custom-call | flops 100000000 | bytes 10000000 | tf_op jit(solution)/shard_map/finish/pallas_call | solution.py:376
  226.3 17.3 %wrap.1 = (f32[2048,1152]{1,0:T(8,128)}, f32[2048,1152]{1,0:T(8,128)}, f32[4,144,1152]{2,1,0:T(8,128)}, f32[4,144,1152]{2,1,0:T(8,128)}, f32[6,72,1152]{2,1,0:T(...) custom-call(bf16[2048,1152]{1,0:T(8,128)(2,1)} %get-tuple-element.94, ...), custom_call_target="tpu_custom_call" | custom-call | flops 1000000000 | bytes 40000000 | tf_op jit(solution)/shard_map/wrap/pallas_call | solution.py:1220
